TPU v7x, 32 devices: a whole 2x2x4 slice. The times are simulated.
32 devices in a mesh: et: 4 (over y, x), ex: 4 (over z), dp: 2 (over core).
Axes of the slice: x: 2, y: 2, z: 4, core: 2. Of those that a mesh axis runs over, the one named last changes fastest.
Arguments:
- tokens: bfloat16 [1024, 1664], P(('et', 'ex', 'dp')), may hold values from -6 to 6
- gate_probs: float32 [1024, 2], P(('et', 'ex', 'dp')), may hold values from 0.2 to 1
- expert_ids: int32 [1024, 2], P(('et', 'ex', 'dp')), may hold values from 0 to 15, as said below
- copies: int32 [16], replicated, may hold values from 1 to 2, as said below
- weight_in: bfloat16 [16, 1664, 8192], P('ex', None, ('et', 'dp')), may hold values from -0.15625 to 0.15625
- weight_out: bfloat16 [16, 8192, 1664], P('ex', ('et', 'dp')), may hold values from -0.0625 to 0.0625
- cotangent: bfloat16 [1024, 1664], P(('et', 'ex', 'dp')), may hold values from -6 to 6
Outputs:
- layer_out: bfloat16 [1024, 1664], P(('et', 'ex', 'dp'))
- grad_tokens: bfloat16 [1024, 1664], P(('et', 'ex', 'dp'))
- grad_gates: float32 [1024, 2], P(('et', 'ex', 'dp'))
- grad_weight_in: float32 [16, 1664, 8192], P('ex', None, ('et', 'dp'))
- grad_weight_out: float32 [16, 8192, 1664], P('ex', ('et', 'dp'))
Inputs may be any that keep to these rules, and one draw needn't show every extreme that they name: `expert_ids`: the two experts of a token differ. Of each aligned run of 4 experts exactly one has 2 copies.
All inputs are finite; a program needn't handle non-finite values.
Results may differ from a plain program's by a relative error of at most 0.02.
Values may be sent and summed in bfloat16 or wider, within the bound.
No kernel may reach another device: no remote copies, remote signals or barrier semaphores. Data moves between devices by JAX's collectives and lax.ppermute only.
A program may use at most 192 MiB of HBM per device.

v0:
```python
import jax
import jax.numpy as jnp
from jax import lax
from jax.experimental import pallas as pl
from jax.experimental.pallas import tpu as pltpu
from jax.sharding import PartitionSpec as P


gelu_scale = 0.7978845608028654
bf16 = jnp.bfloat16
f32 = jnp.float32

ANY = pl.BlockSpec(memory_space=pl.ANY)
VMEM = pl.BlockSpec(memory_space=pltpu.VMEM)
SMEM = pl.BlockSpec(memory_space=pltpu.SMEM)
HBM = pl.BlockSpec(memory_space=pltpu.HBM)


def dot(a, b):
    return lax.dot_general(a, b, (((1,), (0,)), ((), ())), preferred_element_type=f32)


def dot_nt(a, b):
    return lax.dot_general(a, b, (((1,), (1,)), ((), ())), preferred_element_type=f32)


def dot_tn(a, b):
    return lax.dot_general(a, b, (((0,), (0,)), ((), ())), preferred_element_type=f32)


def gelu_tanh(v):
    return 0.5 * v * (1.0 + jnp.tanh(gelu_scale * (v + 0.044715 * v * v * v)))


def gelu_slope(v):
    t = jnp.tanh(gelu_scale * (v + 0.044715 * v * v * v))
    inner = gelu_scale * (1.0 + 3.0 * 0.044715 * v * v)
    return 0.5 * (1.0 + t) + 0.5 * v * (1.0 - t * t) * inner


def call(body, ins, outs, specs_in, specs_out, scratch=(), limit=8, cost=0, aliases=None):
    ins = [
        v if any(spec is s for s in (ANY, SMEM)) else pltpu.with_memory_space_constraint(v, spec.memory_space)
        for v, spec in zip(ins, specs_in)
    ]
    return pl.pallas_call(
        body,
        in_specs=specs_in,
        out_specs=specs_out,
        out_shape=outs,
        scratch_shapes=list(scratch),
        compiler_params=pltpu.CompilerParams(vmem_limit_bytes=limit * 2**20),
        cost_estimate=pl.CostEstimate(flops=0, transcendentals=0, bytes_accessed=cost or 2**20),
        input_output_aliases=aliases or {},
    )(*ins)


def shape(dims, kind):
    return jax.ShapeDtypeStruct(dims, kind)


def token():
    return shape((8, 128), f32)


def log2(n):
    assert n & (n - 1) == 0
    return n.bit_length() - 1


def move(value, axis, size, offset):
    return lax.ppermute(value, axis, [(i, i ^ offset) for i in range(size)])


class Sizes:
    def __init__(self, tokens, weight_in, copies):
        self.et = lax.axis_size("et")
        self.ex = lax.axis_size("ex")
        self.dp = lax.axis_size("dp")
        self.tok, self.d = tokens.shape
        self.experts = copies.shape[0]
        self.gs = self.experts // self.ex
        self.f = weight_in.shape[2]
        self.cap = max(2, self.tok // 16)
        self.nb = self.gs + 1
        self.slots = self.nb * self.cap
        self.frame = -(-2 * self.slots // 8) * 8
        self.rb = self.ex * self.cap
        self.half = self.nb * self.rb
        self.src = self.et * self.dp
        self.rows = self.src * self.rb


def diagonal(n):
    row = lax.broadcasted_iota(jnp.int32, (n, n), 0)
    return row == lax.broadcasted_iota(jnp.int32, (n, n), 1)


def as_column(row):
    return jnp.sum(jnp.where(diagonal(row.shape[1]), row, 0.0), axis=1, keepdims=True)


def as_row(column):
    return jnp.sum(jnp.where(diagonal(column.shape[0]), column, 0.0), axis=0, keepdims=True)


def stack_frames(refs):
    return jnp.concatenate([r[...].astype(f32) for r in refs], axis=0).astype(bf16)


def send_frame(z, tokens, gates, ids, copies, cotangent):
    ins = (tokens, gates, ids, copies.reshape(1, -1), cotangent)

    def body(*refs):
        n = len(ins)
        outs, held, sem = refs[n : n + z.ex + 3], refs[n + z.ex + 3 : -1], refs[-1]
        fetch = [pltpu.make_async_copy(refs[i], held[i], sem.at[i]) for i in range(n)]
        for c in fetch:
            c.start()
        for c in fetch:
            c.wait()
        tok_ref, gate_ref, id_ref, copy_ref, cot_ref = held
        me = lax.axis_index("ex")
        lab = lax.broadcasted_iota(jnp.int32, (z.experts, z.tok), 0)
        hot = [id_ref[k : k + 1, :] == lab for k in range(2)]
        count = (hot[0].astype(f32) + hot[1].astype(f32)).astype(bf16)
        row = lax.broadcasted_iota(jnp.int32, (z.tok, z.tok), 0)
        col = lax.broadcasted_iota(jnp.int32, (z.tok, z.tok), 1)
        earlier = dot(count, (row < col).astype(f32).astype(bf16))
        allow = as_column((copy_ref[...] * z.cap).astype(f32))
        places = lax.broadcasted_iota(jnp.int32, (z.ex * z.frame, z.tok), 0)
        in_tables, up_tables, ups = [], [], []
        cot = cot_ref[...].astype(f32)
        for k in range(2):
            rank = jnp.sum(jnp.where(hot[k], earlier, 0.0), axis=0, keepdims=True)
            limit = jnp.sum(jnp.where(hot[k], allow, 0.0), axis=0, keepdims=True)
            irank = rank.astype(jnp.int32)
            eid = id_ref[k : k + 1, :]
            group = (eid >> log2(z.gs)) ^ me
            within = eid & (z.gs - 1)
            slot = jnp.where(irank < z.cap, within * z.cap, (z.gs - 1) * z.cap) + irank
            target = group * z.frame + slot
            kept = rank < limit
            in_tables.append((jnp.where(kept, target, -1) == places).astype(f32).astype(bf16))
            up_tables.append(
                (jnp.where(kept, target + z.slots, -1) == places).astype(f32).astype(bf16)
            )
            ups.append((as_column(gate_ref[k : k + 1, :]) * cot).astype(bf16))
        sent = dot(in_tables[0] + in_tables[1], tok_ref[...])
        sent = sent + (dot(up_tables[0], ups[0]) + dot(up_tables[1], ups[1]))
        for k in range(z.ex):
            outs[k][...] = sent[k * z.frame : (k + 1) * z.frame].astype(bf16)
        outs[z.ex][...] = in_tables[0]
        outs[z.ex + 1][...] = in_tables[1]
        outs[z.ex + 2][...] = up_tables[0] + up_tables[1]

    outs = [shape((z.frame, z.d), bf16)] * z.ex + [shape((z.ex * z.frame, z.tok), bf16)] * 3
    res = call(
        body,
        ins,
        outs,
        [HBM] * len(ins),
        [VMEM] * len(outs),
        [pltpu.VMEM(v.shape, v.dtype) for v in ins] + [pltpu.SemaphoreType.DMA((len(ins),))],
    )
    return res[: z.ex], res[z.ex :]


def block_select(z):
    dims = (2 * z.half, z.ex * z.frame)
    r = lax.broadcasted_iota(jnp.int32, dims, 0)
    c = lax.broadcasted_iota(jnp.int32, dims, 1)
    upper = r >= z.half
    r = jnp.where(upper, r - z.half, r)
    block = r >> log2(z.rb)
    source = (r & (z.rb - 1)) >> log2(z.cap)
    slot = r & (z.cap - 1)
    want = source * z.frame + block * z.cap + slot + jnp.where(upper, z.slots, 0)
    return (want == c).astype(f32).astype(bf16)


def to_blocks(z, frames, after):
    def body(*refs):
        rows = dot(block_select(z), stack_frames(refs[: z.ex]))
        refs[z.ex + 1][...] = rows[: z.half].astype(bf16)
        refs[z.ex + 2][...] = rows[z.half :].astype(bf16)

    return call(
        body, (*frames, after), [shape((z.half, z.d), bf16)] * 2, [VMEM] * z.ex + [ANY], [VMEM] * 2
    )


def load_weights(weight, after):
    n = weight.shape[0]

    def body(w, _, out, mark, sem):
        copies = [pltpu.make_async_copy(w.at[e], out.at[e], sem.at[e]) for e in range(n)]
        for c in copies:
            c.start()
        mark[...] = jnp.zeros_like(mark)
        for c in copies:
            c.wait()

    return call(
        body,
        (weight, after),
        [shape(weight.shape, weight.dtype), token()],
        [HBM, ANY],
        [VMEM, VMEM],
        [pltpu.SemaphoreType.DMA((n,))],
        cost=2 * weight.size,
    )


def plane_moves(z, own):
    return [own] + [move(own, "et", z.et, m) for m in range(1, z.et)]


def swap_cores(z, mine, after):
    late, _ = lax.optimization_barrier((mine[1:], after))
    mine = [mine[0]] + late
    others = []
    for c in range(1, z.dp):
        others += [move(v, "dp", z.dp, c) for v in mine]
    return mine + others


def assemble(z, refs, out):
    for j in range(z.nb):
        out[j] = jnp.concatenate([r[j * z.rb : (j + 1) * z.rb, :] for r in refs], axis=0)


def scatter_rows(z, value, block, base, refs):
    start = pl.multiple_of(base + block * z.rb, 8)
    for i in range(z.src):
        refs[i // z.et][i % z.et, pl.ds(start, z.rb), :] = value[i * z.rb : (i + 1) * z.rb]


def per_expert(z, copy_ref, work):
    base = lax.axis_index("ex") * z.gs

    def step(e, carry):
        doubled = copy_ref[base + e] > 1

        @pl.when(doubled)
        def _():
            work(e, (e, z.gs))

        @pl.when(jnp.logical_not(doubled))
        def _():
            work(e, (e,))

        return carry

    lax.fori_loop(0, z.gs, step, 0)


def rows_of(ref, blocks):
    if len(blocks) == 1:
        return ref[blocks[0]]
    return jnp.concatenate([ref[b] for b in blocks], axis=0)


def forward_in(z, copies, blocks, weight_in, after):
    def body(copy_ref, *refs):
        srcs = refs[: z.src]
        w, _, xall, pre, hid, mark = refs[z.src :]
        mark[...] = jnp.zeros_like(mark)
        assemble(z, srcs, xall)

        def work(e, ids):
            v = dot(rows_of(xall, ids), w[e])
            h = gelu_tanh(v).astype(bf16)
            for i, b in enumerate(ids):
                pre[b] = v[i * z.rows : (i + 1) * z.rows]
                hid[b] = h[i * z.rows : (i + 1) * z.rows]

        per_expert(z, copy_ref, work)

    return call(
        body,
        (copies, *blocks, weight_in, after),
        [
            shape((z.nb, z.rows, z.d), bf16),
            shape((z.nb, z.rows, z.f), f32),
            shape((z.nb, z.rows, z.f), bf16),
            token(),
        ],
        [SMEM] + [VMEM] * (z.src + 2),
        [VMEM] * 4,
        cost=16 * 2**20,
    )


def middle(z, copies, blocks, weight_in, weight_out, pre, hid):
    def body(copy_ref, *refs):
        srcs = refs[: z.src]
        win, wout, pre_ref, hid_ref, uall, slope, *outs = refs[z.src :]
        assemble(z, srcs, uall)

        def work(e, ids):
            back = dot_nt(rows_of(uall, ids), wout[e])
            s = (back * gelu_slope(rows_of(pre_ref, ids))).astype(bf16)
            o = dot(rows_of(hid_ref, ids), wout[e]).astype(bf16)
            g = dot_nt(s, win[e]).astype(bf16)
            for i, b in enumerate(ids):
                part = slice(i * z.rows, (i + 1) * z.rows)
                slope[b] = s[part]
                scatter_rows(z, o[part], b, 0, outs)
                scatter_rows(z, g[part], b, z.half, outs)

        per_expert(z, copy_ref, work)

    res = call(
        body,
        (copies, *blocks, weight_in, weight_out, pre, hid),
        [shape((z.nb, z.rows, z.d), bf16), shape((z.nb, z.rows, z.f), bf16)]
        + [shape((z.et, 2 * z.half, z.d), bf16)] * z.dp,
        [SMEM] + [VMEM] * (z.src + 4),
        [VMEM] * (2 + z.dp),
        cost=48 * 2**20,
    )
    return res[0], res[1], res[2:]


def weight_grads(z, copies, rows, jobs, held, after):
    kinds = [which for which, _, _ in jobs]
    operands, spans, alias = [], [], {}
    for which in kinds:
        operands += list(rows[which])
    for which in kinds:
        tiles = rows[which][0].shape[2] // 128
        edge = (tiles + 1) // 2 * 128
        spans.append(((0, edge), (edge, tiles * 128 - edge)))
    parts = 2
    old = [held[which] for which in kinds if held[which] is not None]
    at = 1 + len(operands)
    for i, which in enumerate(kinds):
        if held[which] is not None:
            alias[at] = i
            at += 1

    def body(copy_ref, *refs):
        ins = refs[: len(operands)]
        outs = refs[len(operands) + len(old) + 1 :]
        mark = outs[len(jobs)]
        sems = outs[-1]
        mark[...] = jnp.zeros_like(mark)
        base = lax.axis_index("ex") * z.gs

        def copy_of(i, e, p):
            start, size = spans[i][p]
            src = outs[len(jobs) + 1 + i].at[pl.ds(start, size), :]
            return pltpu.make_async_copy(src, outs[i].at[e, pl.ds(start, size), :], sems.at[i, p])

        def work(i, first, e, ids):
            left, right = ins[2 * i], ins[2 * i + 1]
            buf = outs[len(jobs) + 1 + i]
            r = rows_of(right, ids)
            for p, (start, size) in enumerate(spans[i]):
                l = [left[b, :, start : start + size] for b in ids]
                v = dot_tn(l[0] if len(ids) == 1 else jnp.concatenate(l, axis=0), r)

                @pl.when(e > first)
                def _():
                    copy_of(i, e - 1, p).wait()

                buf[start : start + size, :] = v
                copy_of(i, e, p).start()

        for i, (which, first, last) in enumerate(jobs):

            def step(e, carry):
                doubled = copy_ref[base + e] > 1

                @pl.when(doubled)
                def _():
                    work(i, first, e, (e, z.gs))

                @pl.when(jnp.logical_not(doubled))
                def _():
                    work(i, first, e, (e,))

                return carry

            lax.fori_loop(first, last, step, 0)
        for i, (which, first, last) in enumerate(jobs):
            for p in range(parts):
                copy_of(i, last - 1, p).wait()

    outs = [
        pltpu.HBM((z.gs, rows[which][0].shape[2], rows[which][1].shape[2]), f32)
        for which in kinds
    ]
    res = call(
        body,
        (copies, *operands, *old, after),
        outs + [token()],
        [SMEM] + [VMEM] * len(operands) + [HBM] * len(old) + [ANY],
        [HBM] * len(jobs) + [VMEM],
        [pltpu.VMEM((rows[w][0].shape[2], rows[w][1].shape[2]), f32) for w in kinds]
        + [pltpu.SemaphoreType.DMA((len(jobs), parts))],
        limit=24,
        cost=4 * sum((last - first) * rows[w][0].shape[2] * rows[w][1].shape[2] for w, first, last in jobs),
        aliases=alias,
    )
    held = list(held)
    for i, which in enumerate(kinds):
        held[which] = res[i]
    return held, res[-1]


def pair_sum(z, own, got, after):
    def body(*refs):
        for m in range(z.et):
            total = refs[0][m].astype(f32)
            for c in range(1, z.dp):
                total = total + refs[c][m].astype(f32)
            refs[z.dp + 1 + m][...] = total.astype(bf16)

    return call(
        body,
        (own, *got, after),
        [shape((2 * z.half, z.d), bf16)] * z.et,
        [VMEM] * z.dp + [ANY],
        [VMEM] * z.et,
    )


def to_frames(z, parts, after):
    def body(*refs):
        total = refs[0][...].astype(f32)
        for m in range(1, z.et):
            total = total + refs[m][...].astype(f32)
        frames = dot_tn(block_select(z), total.astype(bf16))
        for k in range(z.ex):
            refs[z.et + 1 + k][...] = frames[k * z.frame : (k + 1) * z.frame].astype(bf16)

    return call(
        body,
        (*parts, after),
        [shape((z.frame, z.d), bf16)] * z.ex,
        [VMEM] * z.et + [ANY],
        [VMEM] * z.ex,
    )


def combine(z, gates, cotangent, tables, frames, after):
    def body(gate_ref, cot_ref, t0, t1, t2, *refs):
        rows = stack_frames(refs[: z.ex])
        layer_ref, gtok_ref, ggate_ref = refs[z.ex + 1 :]
        cot = cot_ref[...].astype(f32)
        p0 = dot_tn(t0[...], rows)
        p1 = dot_tn(t1[...], rows)
        gate0 = as_column(gate_ref[0:1, :])
        gate1 = as_column(gate_ref[1:2, :])
        layer_ref[...] = (gate0 * p0 + gate1 * p1).astype(bf16)
        ggate_ref[0:1, :] = as_row(jnp.sum(cot * p0, axis=1, keepdims=True))
        ggate_ref[1:2, :] = as_row(jnp.sum(cot * p1, axis=1, keepdims=True))
        gtok_ref[...] = dot_tn(t2[...], rows).astype(bf16)

    return call(
        body,
        (gates, cotangent, *tables, *frames, after),
        [shape((z.tok, z.d), bf16), shape((z.tok, z.d), bf16), shape((2, z.tok), f32)],
        [VMEM] * (5 + z.ex) + [ANY],
        [VMEM] * 3,
    )


def shards(tokens, gate_probs, expert_ids, copies, weight_in, weight_out, cotangent):
    z = Sizes(tokens, weight_in, copies)
    gates = gate_probs.T
    frames, tables = send_frame(z, tokens, gates, expert_ids.T, copies, cotangent)
    got = [frames[0]] + [move(frames[k], "ex", z.ex, k) for k in range(1, z.ex)]
    win, mark = load_weights(weight_in, frames[0])
    own_x, own_u = to_blocks(z, got, mark)
    mine_x = plane_moves(z, own_x)
    mine_u = plane_moves(z, own_u)
    wout, mark = load_weights(weight_out, own_x)
    blocks_x = swap_cores(z, mine_x, mark)
    xall, pre, hid, mark = forward_in(z, copies, blocks_x, win, wout)
    blocks_u = swap_cores(z, mine_u, mark)
    uall, slope, parts = middle(z, copies, blocks_u, win, wout, pre, hid)
    pairs = ((hid, uall), (xall, slope))
    held = [None, None]
    swapped = [move(parts[c], "dp", z.dp, c) for c in range(1, z.dp)]
    held, mark = weight_grads(z, copies, pairs, [(0, 0, 1)], held, parts[1])
    sums = pair_sum(z, parts[0], swapped, mark)
    parts = [sums[0]] + [move(sums[m], "et", z.et, m) for m in range(1, z.et)]
    held, mark = weight_grads(z, copies, pairs, [(0, 1, z.gs), (1, 0, 1)], held, sums[0])
    frames = to_frames(z, parts, mark)
    frames = [frames[0]] + [move(frames[k], "ex", z.ex, k) for k in range(1, z.ex)]
    held, mark = weight_grads(z, copies, pairs, [(1, 1, z.gs)], held, frames[0])
    grad_weight_out, grad_weight_in = held
    layer_out, grad_tokens, grad_gates = combine(z, gates, cotangent, tables, frames, mark)
    return (layer_out, grad_tokens, grad_gates.T, grad_weight_in, grad_weight_out)


def solution(mesh):
    rows = P(("et", "ex", "dp"), None)
    w_in = P("ex", None, ("et", "dp"))
    w_out = P("ex", ("et", "dp"), None)
    return jax.shard_map(
        shards,
        mesh=mesh,
        in_specs=(rows, rows, rows, P(), w_in, w_out, rows),
        out_specs=(rows, rows, rows, w_in, w_out),
        check_vma=False,
    )
```

profile of v0, /device:TPU:0, one launch (start us, length us, event | category | flops | bytes accessed | tf_op | source)
XLA Modules:
  0.0 85.6 jit_solution(17578879299709854775)
XLA Ops:
  0.6 1.6 %shard_map.110 = (bf16[24,1664]{1,0:T(8,128)(2,1)S(1)}, bf16[24,1664]{1,0:T(8,128)(2,1)S(1)}, bf16[24,1664]{1,0:T(8,128)(2,1)S(1)}, bf16[24,1664]{1,0:T(8,128)(2...) custom-call(bf16[32,1664]{1,0:T(8,128)(2,1)} %refs_0_.1, ...), custom_call_target="tpu_custom_call" | custom-call | bytes 1048576 | tf_op jit(solution)/shard_map/pallas_call | solution.py:46
  2.2 3.1 %collective-permute-start = (bf16[24,1664]{1,0:T(8,128)(2,1)S(1)}, bf16[24,1664]{1,0:T(8,128)(2,1)S(1)}, u32[]{:S(2)}, u32[]{:S(2)}) collective-permute-start(bf16[24,1664]{1,0:T(8,128)(2,1)S(1)} %get-tuple-element.52), channel_id=1, source_target_pairs={{0,2},{2,0},{4,6},{6,4},{1,3},{3,1},{5,7},{7,5},{8,10},{10,8},{12,... | collective-permute-start | bytes 239624 | tf_op jit(solution)/shard_map/ppermute | solution.py:72
  5.3 2.6 %collective-permute-start.1 = (bf16[24,1664]{1,0:T(8,128)(2,1)S(1)}, bf16[24,1664]{1,0:T(8,128)(2,1)S(1)}, u32[]{:S(2)}, u32[]{:S(2)}) collective-permute-start(bf16[24,1664]{1,0:T(8,128)(2,1)S(1)} %get-tuple-element.53), channel_id=1, source_target_pairs={{0,4},{2,6},{4,0},{6,2},{1,5},{3,7},{5,1},{7,3},{8,12},{10,14},{12... | collective-permute-start | bytes 239624 | tf_op jit(solution)/shard_map/ppermute | solution.py:72
  7.9 5.0 %shard_map.111 = (bf16[4,1664,1024]{2,1,0:T(8,128)(2,1)S(1)}, f32[8,128]{1,0:T(8,128)S(1)}) custom-call(bf16[4,1664,1024]{2,1,0:T(8,128)(2,1)} %w.2, bf16[24,1664]{1,0:T(8,128)(2,1)S(1)} %get-tuple-element.51._.refs_0_), custom_call_target="tpu_custom_call" | custom-call | bytes 13631488 | tf_op jit(solution)/shard_map/pallas_call | solution.py:46
  12.9 1.4 %collective-permute-done.1.refs_2_ = bf16[24,1664]{1,0:T(8,128)(2,1)S(1)} collective-permute-done((bf16[24,1664]{1,0:T(8,128)(2,1)S(1)}, bf16[24,1664]{1,0:T(8,128)(2,1)S(1)}, u32[]{:S(2)}, u32[]{:S(2)}) %collective-permute-start.1) | collective-permute-done | bytes 79904 | tf_op jit(solution)/shard_map/ppermute | solution.py:72
  14.6 2.5 %collective-permute-start.12 = (bf16[40,1664]{1,0:T(8,128)(2,1)S(1)}, bf16[40,1664]{1,0:T(8,128)(2,1)S(1)}, u32[]{:S(2)}, u32[]{:S(2)}) collective-permute-start(bf16[40,1664]{1,0:T(8,128)(2,1)S(1)} %get-tuple-element.61._.refs_0_), channel_id=1, source_target_pairs={{0,24},{8,16},{16,8},{24,0},{1,25},{9,17},{17,9},{25,1},{2,26},{10... | collective-permute-start | bytes 399368 | tf_op jit(solution)/shard_map/ppermute | solution.py:72
  18.1 2.5 %collective-permute-start.5 = (bf16[40,1664]{1,0:T(8,128)(2,1)S(1)}, bf16[40,1664]{1,0:T(8,128)(2,1)S(1)}, u32[]{:S(2)}, u32[]{:S(2)}) collective-permute-start(bf16[40,1664]{1,0:T(8,128)(2,1)S(1)} %get-tuple-element.56.refs_0_), channel_id=1, source_target_pairs={{0,24},{8,16},{16,8},{24,0},{1,25},{9,17},{17,9},{25,1},{2,26},{10... | collective-permute-start | bytes 399368 | tf_op jit(solution)/shard_map/ppermute | solution.py:72
  21.1 1.0 %collective-permute-done.12.refs_3_ = bf16[40,1664]{1,0:T(8,128)(2,1)S(1)} collective-permute-done((bf16[40,1664]{1,0:T(8,128)(2,1)S(1)}, bf16[40,1664]{1,0:T(8,128)(2,1)S(1)}, u32[]{:S(2)}, u32[]{:S(2)}) %collective-permute-start.12) | collective-permute-done | bytes 133152 | tf_op jit(solution)/shard_map/ppermute | solution.py:72
  22.1 1.4 %collective-permute-start.3 = (bf16[40,1664]{1,0:T(8,128)(2,1)S(1)}, bf16[40,1664]{1,0:T(8,128)(2,1)S(1)}, u32[]{:S(2)}, u32[]{:S(2)}) collective-permute-start(bf16[40,1664]{1,0:T(8,128)(2,1)S(1)} %get-tuple-element.56.refs_0_), channel_id=1, source_target_pairs={{0,8},{8,0},{16,24},{24,16},{1,9},{9,1},{17,25},{25,17},{2,10},{10... | collective-permute-start | bytes 399368 | tf_op jit(solution)/shard_map/ppermute | solution.py:72
  23.5 2.0 %collective-permute-done.11.refs_2_ = bf16[40,1664]{1,0:T(8,128)(2,1)S(1)} collective-permute-done((bf16[40,1664]{1,0:T(8,128)(2,1)S(1)}, bf16[40,1664]{1,0:T(8,128)(2,1)S(1)}, u32[]{:S(2)}, u32[]{:S(2)}) %collective-permute-start.11) | collective-permute-done | bytes 133152 | tf_op jit(solution)/shard_map/ppermute | solution.py:72
  26.1 1.2 %collective-permute-done.5.refs_3_ = bf16[40,1664]{1,0:T(8,128)(2,1)S(1)} collective-permute-done((bf16[40,1664]{1,0:T(8,128)(2,1)S(1)}, bf16[40,1664]{1,0:T(8,128)(2,1)S(1)}, u32[]{:S(2)}, u32[]{:S(2)}) %collective-permute-start.5) | collective-permute-done | bytes 133152 | tf_op jit(solution)/shard_map/ppermute | solution.py:72
  27.2 0.9 %collective-permute-done.4.refs_2_ = bf16[40,1664]{1,0:T(8,128)(2,1)S(1)} collective-permute-done((bf16[40,1664]{1,0:T(8,128)(2,1)S(1)}, bf16[40,1664]{1,0:T(8,128)(2,1)S(1)}, u32[]{:S(2)}, u32[]{:S(2)}) %collective-permute-start.4) | collective-permute-done | bytes 133152 | tf_op jit(solution)/shard_map/ppermute | solution.py:72
  29.2 5.6 %shard_map.113 = (bf16[4,1024,1664]{2,1,0:T(8,128)(2,1)S(1)}, f32[8,128]{1,0:T(8,128)}) custom-call(bf16[4,1024,1664]{2,1,0:T(8,128)(2,1)} %w.3, bf16[40,1664]{1,0:T(8,128)(2,1)S(1)} %get-tuple-element.61._.refs_0_), custom_call_target="tpu_custom_call" | custom-call | bytes 13631488 | tf_op jit(solution)/shard_map/pallas_call | solution.py:46
  34.8 4.4 %shard_map.114 = (bf16[5,64,1664]{2,1,0:T(8,128)(2,1)S(1)}, f32[5,64,1024]{2,1,0:T(8,128)S(1)}, bf16[5,64,1024]{2,1,0:T(8,128)(2,1)S(1)}, f32[8,128]{1,0:T(8,128)}) custom-call(s32[16]{0:T(128)S(1)} %copy-done.1, bf16[40,1664]{1,0:T(8,128)(2,1)S(1)} %get-tuple-element.61._.refs_0_, bf16[40,1664]{1,0:T(8,128)(2,1)S(1)} %collective-permute-done.10.refs_1_, ...), custom_call_target="tpu_custom_call" | custom-call | bytes 16777216 | tf_op jit(solution)/shard_map/pallas_call | solution.py:46
  39.2 11.8 %shard_map.115 = (bf16[5,64,1664]{2,1,0:T(8,128)(2,1)S(1)}, bf16[5,64,1024]{2,1,0:T(8,128)(2,1)S(1)}, bf16[4,80,1664]{2,1,0:T(8,128)(2,1)S(1)}, bf16[4,80,1664]{2,1,0:T(8,128)(2,1)S(1)}) custom-call(s32[16]{0:T(128)S(1)} %copy-done.1, bf16[40,1664]{1,0:T(8,128)(2,1)S(1)} %get-tuple-element.56.refs_0_, bf16[40,1664]{1,0:T(8,128)(2,1)S(1)} %collective-permute-done.3.refs_1_, ...), custom_call_target="tpu_custom_call" | custom-call | bytes 50331648 | tf_op jit(solution)/shard_map/pallas_call | solution.py:46
  51.6 4.1 %shard_map.116 = (f32[4,1024,1664]{2,1,0:T(8,128)}, f32[8,128]{1,0:T(8,128)S(1)}) custom-call(s32[16]{0:T(128)S(1)} %copy-done.1, bf16[5,64,1024]{2,1,0:T(8,128)(2,1)S(1)} %get-tuple-element.67.refs_11_.refs_0_, bf16[5,64,1664]{2,1,0:T(8,128)(2,1)S(1)} %get-tuple-element.70.refs_1_, bf16[4,80,1664]{2,1,0:T(8,128)(2,1)S(1)} %get-tuple-element.69.refs_2_), custom_call_target="tpu_custom_call" | custom-call | bytes 6815744 | tf_op jit(solution)/shard_map/pallas_call | solution.py:46
  55.9 1.0 %collective-permute-start.18 = (bf16[80,1664]{1,0:T(8,128)(2,1)S(1)}, bf16[80,1664]{1,0:T(8,128)(2,1)S(1)}, u32[]{:S(2)}, u32[]{:S(2)}) collective-permute-start(bf16[80,1664]{1,0:T(8,128)(2,1)S(1)} %get-tuple-element.73), channel_id=1, source_target_pairs={{0,8},{8,0},{16,24},{24,16},{1,9},{9,1},{17,25},{25,17},{2,10},{10... | collective-permute-start | bytes 798728 | tf_op jit(solution)/shard_map/ppermute | solution.py:72
  57.7 1.8 %collective-permute-start.20 = (bf16[80,1664]{1,0:T(8,128)(2,1)S(1)}, bf16[80,1664]{1,0:T(8,128)(2,1)S(1)}, u32[]{:S(2)}, u32[]{:S(2)}) collective-permute-start(bf16[80,1664]{1,0:T(8,128)(2,1)S(1)} %get-tuple-element.75), channel_id=1, source_target_pairs={{0,24},{8,16},{16,8},{24,0},{1,25},{9,17},{17,9},{25,1},{2,26},{10... | collective-permute-start | bytes 798728 | tf_op jit(solution)/shard_map/ppermute | solution.py:72
  59.5 10.6 %shard_map.118 = (f32[4,1024,1664]{2,1,0:T(8,128)}, f32[4,1664,1024]{2,1,0:T(8,128)}, f32[8,128]{1,0:T(8,128)S(1)}) custom-call(s32[16]{0:T(128)S(1)} %copy-done.1, bf16[5,64,1024]{2,1,0:T(8,128)(2,1)S(1)} %get-tuple-element.67.refs_11_.refs_0_, bf16[5,64,1664]{2,1,0:T(8,128)(2,1)S(1)} %get-tuple-element.70.refs_1_, ...), custom_call_target="tpu_custom_call", output_to_operand_aliasing={{0}: (5, {})} | custom-call | bytes 27262976 | tf_op jit(solution)/shard_map/pallas_call | solution.py:46
  71.1 2.4 %collective-permute-start.21 = (bf16[24,1664]{1,0:T(8,128)(2,1)S(1)}, bf16[24,1664]{1,0:T(8,128)(2,1)S(1)}, u32[]{:S(2)}, u32[]{:S(2)}) collective-permute-start(bf16[24,1664]{1,0:T(8,128)(2,1)S(1)} %get-tuple-element.81), channel_id=1, source_target_pairs={{0,2},{2,0},{4,6},{6,4},{1,3},{3,1},{5,7},{7,5},{8,10},{10,8},{12,... | collective-permute-start | bytes 239624 | tf_op jit(solution)/shard_map/ppermute | solution.py:72
  73.5 1.6 %collective-permute-start.22 = (bf16[24,1664]{1,0:T(8,128)(2,1)S(1)}, bf16[24,1664]{1,0:T(8,128)(2,1)S(1)}, u32[]{:S(2)}, u32[]{:S(2)}) collective-permute-start(bf16[24,1664]{1,0:T(8,128)(2,1)S(1)} %get-tuple-element.82), channel_id=1, source_target_pairs={{0,4},{2,6},{4,0},{6,2},{1,5},{3,7},{5,1},{7,3},{8,12},{10,14},{12... | collective-permute-start | bytes 239624 | tf_op jit(solution)/shard_map/ppermute | solution.py:72
  75.2 0.8 collective-permute-start.23
  76.0 8.6 %shard_map.120 = (f32[4,1664,1024]{2,1,0:T(8,128)}, f32[8,128]{1,0:T(8,128)S(1)}) custom-call(s32[16]{0:T(128)S(1)} %copy-done.1, bf16[5,64,1664]{2,1,0:T(8,128)(2,1)S(1)} %get-tuple-element.76.refs_2_.refs_0_, bf16[5,64,1024]{2,1,0:T(8,128)(2,1)S(1)} %get-tuple-element.77.refs_3_.refs_1_, ...), custom_call_target="tpu_custom_call", output_to_operand_aliasing={{0}: (3, {})} | custom-call | bytes 20447232 | tf_op jit(solution)/shard_map/pallas_call | solution.py:46
  84.6 1.0 %shard_map.121 = (bf16[32,1664]{1,0:T(8,128)(2,1)}, bf16[32,1664]{1,0:T(8,128)(2,1)}, f32[2,32]{1,0:T(2,128)}) custom-call(f32[2,32]{1,0:T(2,128)S(1)} %bitcast.6, bf16[32,1664]{1,0:T(8,128)(2,1)S(1)} %copy-done, bf16[96,32]{1,0:T(8,128)(2,1)S(1)} %get-tuple-element.48.t0, bf16[96,32]{1,0:T(8,128)(2,1)S(1)} %get-tuple-element.49.t1, ...), custom_call_target="tpu_custom_call" | custom-call | bytes 1048576 | tf_op jit(solution)/shard_map/pallas_call | solution.py:46
  (42 shorter events, 5.9 us)
Async XLA Ops:
  2.2 10.7 %collective-permute-start = (bf16[24,1664]{1,0:T(8,128)(2,1)S(1)}, bf16[24,1664]{1,0:T(8,128)(2,1)S(1)}, u32[]{:S(2)}, u32[]{:S(2)}) collective-permute-start(bf16[24,1664]{1,0:T(8,128)(2,1)S(1)} %get-tuple-element.52), channel_id=1, source_target_pairs={{0,2},{2,0},{4,6},{6,4},{1,3},{3,1},{5,7},{7,5},{8,10},{10,8},{12,... | collective-permute-start | bytes 239624 | tf_op jit(solution)/shard_map/ppermute | solution.py:72
  5.3 9.0 %collective-permute-start.1 = (bf16[24,1664]{1,0:T(8,128)(2,1)S(1)}, bf16[24,1664]{1,0:T(8,128)(2,1)S(1)}, u32[]{:S(2)}, u32[]{:S(2)}) collective-permute-start(bf16[24,1664]{1,0:T(8,128)(2,1)S(1)} %get-tuple-element.53), channel_id=1, source_target_pairs={{0,4},{2,6},{4,0},{6,2},{1,5},{3,7},{5,1},{7,3},{8,12},{10,14},{12... | collective-permute-start | bytes 239624 | tf_op jit(solution)/shard_map/ppermute | solution.py:72
  7.9 6.5 %collective-permute-start.2 = (bf16[24,1664]{1,0:T(8,128)(2,1)S(1)}, bf16[24,1664]{1,0:T(8,128)(2,1)S(1)}, u32[]{:S(2)}, u32[]{:S(2)}) collective-permute-start(bf16[24,1664]{1,0:T(8,128)(2,1)S(1)} %get-tuple-element.54), channel_id=1, source_target_pairs={{0,6},{2,4},{4,2},{6,0},{1,7},{3,5},{5,3},{7,1},{8,14},{10,12},{12... | collective-permute-start | bytes 239624 | tf_op jit(solution)/shard_map/ppermute | solution.py:72
  14.6 7.5 %collective-permute-start.12 = (bf16[40,1664]{1,0:T(8,128)(2,1)S(1)}, bf16[40,1664]{1,0:T(8,128)(2,1)S(1)}, u32[]{:S(2)}, u32[]{:S(2)}) collective-permute-start(bf16[40,1664]{1,0:T(8,128)(2,1)S(1)} %get-tuple-element.61._.refs_0_), channel_id=1, source_target_pairs={{0,24},{8,16},{16,8},{24,0},{1,25},{9,17},{17,9},{25,1},{2,26},{10... | collective-permute-start | bytes 399368 | tf_op jit(solution)/shard_map/ppermute | solution.py:72
  17.1 8.4 %collective-permute-start.11 = (bf16[40,1664]{1,0:T(8,128)(2,1)S(1)}, bf16[40,1664]{1,0:T(8,128)(2,1)S(1)}, u32[]{:S(2)}, u32[]{:S(2)}) collective-permute-start(bf16[40,1664]{1,0:T(8,128)(2,1)S(1)} %get-tuple-element.61._.refs_0_), channel_id=1, source_target_pairs={{0,16},{8,24},{16,0},{24,8},{1,17},{9,25},{17,1},{25,9},{2,18},{10... | collective-permute-start | bytes 399368 | tf_op jit(solution)/shard_map/ppermute | solution.py:72
  17.6 7.9 %collective-permute-start.10 = (bf16[40,1664]{1,0:T(8,128)(2,1)S(1)}, bf16[40,1664]{1,0:T(8,128)(2,1)S(1)}, u32[]{:S(2)}, u32[]{:S(2)}) collective-permute-start(bf16[40,1664]{1,0:T(8,128)(2,1)S(1)} %get-tuple-element.61._.refs_0_), channel_id=1, source_target_pairs={{0,8},{8,0},{16,24},{24,16},{1,9},{9,1},{17,25},{25,17},{2,10},{10... | collective-permute-start | bytes 399368 | tf_op jit(solution)/shard_map/ppermute | solution.py:72
  18.1 9.1 %collective-permute-start.5 = (bf16[40,1664]{1,0:T(8,128)(2,1)S(1)}, bf16[40,1664]{1,0:T(8,128)(2,1)S(1)}, u32[]{:S(2)}, u32[]{:S(2)}) collective-permute-start(bf16[40,1664]{1,0:T(8,128)(2,1)S(1)} %get-tuple-element.56.refs_0_), channel_id=1, source_target_pairs={{0,24},{8,16},{16,8},{24,0},{1,25},{9,17},{17,9},{25,1},{2,26},{10... | collective-permute-start | bytes 399368 | tf_op jit(solution)/shard_map/ppermute | solution.py:72
  20.6 7.5 %collective-permute-start.4 = (bf16[40,1664]{1,0:T(8,128)(2,1)S(1)}, bf16[40,1664]{1,0:T(8,128)(2,1)S(1)}, u32[]{:S(2)}, u32[]{:S(2)}) collective-permute-start(bf16[40,1664]{1,0:T(8,128)(2,1)S(1)} %get-tuple-element.56.refs_0_), channel_id=1, source_target_pairs={{0,16},{8,24},{16,0},{24,8},{1,17},{9,25},{17,1},{25,9},{2,18},{10... | collective-permute-start | bytes 399368 | tf_op jit(solution)/shard_map/ppermute | solution.py:72
  22.1 6.1 %collective-permute-start.3 = (bf16[40,1664]{1,0:T(8,128)(2,1)S(1)}, bf16[40,1664]{1,0:T(8,128)(2,1)S(1)}, u32[]{:S(2)}, u32[]{:S(2)}) collective-permute-start(bf16[40,1664]{1,0:T(8,128)(2,1)S(1)} %get-tuple-element.56.refs_0_), channel_id=1, source_target_pairs={{0,8},{8,0},{16,24},{24,16},{1,9},{9,1},{17,25},{25,17},{2,10},{10... | collective-permute-start | bytes 399368 | tf_op jit(solution)/shard_map/ppermute | solution.py:72
  25.5 3.1 %collective-permute-start.13 = (bf16[40,1664]{1,0:T(8,128)(2,1)S(1)}, bf16[40,1664]{1,0:T(8,128)(2,1)S(1)}, u32[]{:S(2)}, u32[]{:S(2)}) collective-permute-start(bf16[40,1664]{1,0:T(8,128)(2,1)S(1)} %get-tuple-element.61._.refs_0_), channel_id=1, source_target_pairs={{0,1},{1,0},{2,3},{3,2},{4,5},{5,4},{6,7},{7,6},{8,9},{9,8},{10,11... | collective-permute-start | bytes 399368 | tf_op jit(solution)/shard_map/ppermute | solution.py:72
  25.5 3.2 %collective-permute-start.14 = (bf16[40,1664]{1,0:T(8,128)(2,1)S(1)}, bf16[40,1664]{1,0:T(8,128)(2,1)S(1)}, u32[]{:S(2)}, u32[]{:S(2)}) collective-permute-start(bf16[40,1664]{1,0:T(8,128)(2,1)S(1)} %collective-permute-done.10.refs_1_), channel_id=1, source_target_pairs={{0,1},{1,0},{2,3},{3,2},{4,5},{5,4},{6,7},{7,6},{8,9},{9,8},{10,11... | collective-permute-start | bytes 399368 | tf_op jit(solution)/shard_map/ppermute | solution.py:72
  27.2 1.9 %collective-permute-start.15 = (bf16[40,1664]{1,0:T(8,128)(2,1)S(1)}, bf16[40,1664]{1,0:T(8,128)(2,1)S(1)}, u32[]{:S(2)}, u32[]{:S(2)}) collective-permute-start(bf16[40,1664]{1,0:T(8,128)(2,1)S(1)} %collective-permute-done.11.refs_2_), channel_id=1, source_target_pairs={{0,1},{1,0},{2,3},{3,2},{4,5},{5,4},{6,7},{7,6},{8,9},{9,8},{10,11... | collective-permute-start | bytes 399368 | tf_op jit(solution)/shard_map/ppermute | solution.py:72
  28.1 11.1 %collective-permute-start.6 = (bf16[40,1664]{1,0:T(8,128)(2,1)S(1)}, bf16[40,1664]{1,0:T(8,128)(2,1)S(1)}, u32[]{:S(2)}, u32[]{:S(2)}) collective-permute-start(bf16[40,1664]{1,0:T(8,128)(2,1)S(1)} %get-tuple-element.56.refs_0_), channel_id=1, source_target_pairs={{0,1},{1,0},{2,3},{3,2},{4,5},{5,4},{6,7},{7,6},{8,9},{9,8},{10,11... | collective-permute-start | bytes 399368 | tf_op jit(solution)/shard_map/ppermute | solution.py:72
  28.1 6.7 %collective-permute-start.16 = (bf16[40,1664]{1,0:T(8,128)(2,1)S(1)}, bf16[40,1664]{1,0:T(8,128)(2,1)S(1)}, u32[]{:S(2)}, u32[]{:S(2)}) collective-permute-start(bf16[40,1664]{1,0:T(8,128)(2,1)S(1)} %collective-permute-done.12.refs_3_), channel_id=1, source_target_pairs={{0,1},{1,0},{2,3},{3,2},{4,5},{5,4},{6,7},{7,6},{8,9},{9,8},{10,11... | collective-permute-start | bytes 399368 | tf_op jit(solution)/shard_map/ppermute | solution.py:72
  28.6 10.6 %collective-permute-start.7 = (bf16[40,1664]{1,0:T(8,128)(2,1)S(1)}, bf16[40,1664]{1,0:T(8,128)(2,1)S(1)}, u32[]{:S(2)}, u32[]{:S(2)}) collective-permute-start(bf16[40,1664]{1,0:T(8,128)(2,1)S(1)} %collective-permute-done.3.refs_1_), channel_id=1, source_target_pairs={{0,1},{1,0},{2,3},{3,2},{4,5},{5,4},{6,7},{7,6},{8,9},{9,8},{10,11... | collective-permute-start | bytes 399368 | tf_op jit(solution)/shard_map/ppermute | solution.py:72
  28.7 10.5 %collective-permute-start.8 = (bf16[40,1664]{1,0:T(8,128)(2,1)S(1)}, bf16[40,1664]{1,0:T(8,128)(2,1)S(1)}, u32[]{:S(2)}, u32[]{:S(2)}) collective-permute-start(bf16[40,1664]{1,0:T(8,128)(2,1)S(1)} %collective-permute-done.4.refs_2_), channel_id=1, source_target_pairs={{0,1},{1,0},{2,3},{3,2},{4,5},{5,4},{6,7},{7,6},{8,9},{9,8},{10,11... | collective-permute-start | bytes 399368 | tf_op jit(solution)/shard_map/ppermute | solution.py:72
  29.1 10.1 %collective-permute-start.9 = (bf16[40,1664]{1,0:T(8,128)(2,1)S(1)}, bf16[40,1664]{1,0:T(8,128)(2,1)S(1)}, u32[]{:S(2)}, u32[]{:S(2)}) collective-permute-start(bf16[40,1664]{1,0:T(8,128)(2,1)S(1)} %collective-permute-done.5.refs_3_), channel_id=1, source_target_pairs={{0,1},{1,0},{2,3},{3,2},{4,5},{5,4},{6,7},{7,6},{8,9},{9,8},{10,11... | collective-permute-start | bytes 399368 | tf_op jit(solution)/shard_map/ppermute | solution.py:72
  51.1 4.6 %collective-permute-start.17 = (bf16[4,80,1664]{2,1,0:T(8,128)(2,1)S(1)}, bf16[4,80,1664]{2,1,0:T(8,128)(2,1)S(1)}, u32[]{:S(2)}, u32[]{:S(2)}) collective-permute-start(bf16[4,80,1664]{2,1,0:T(8,128)(2,1)S(1)} %get-tuple-element.69.refs_2_), channel_id=1, source_target_pairs={{0,1},{1,0},{2,3},{3,2},{4,5},{5,4},{6,7},{7,6},{8,9},{9,8},{10,11... | collective-permute-start | bytes 3194888 | tf_op jit(solution)/shard_map/ppermute | solution.py:72
  55.9 14.2 %collective-permute-start.18 = (bf16[80,1664]{1,0:T(8,128)(2,1)S(1)}, bf16[80,1664]{1,0:T(8,128)(2,1)S(1)}, u32[]{:S(2)}, u32[]{:S(2)}) collective-permute-start(bf16[80,1664]{1,0:T(8,128)(2,1)S(1)} %get-tuple-element.73), channel_id=1, source_target_pairs={{0,8},{8,0},{16,24},{24,16},{1,9},{9,1},{17,25},{25,17},{2,10},{10... | collective-permute-start | bytes 798728 | tf_op jit(solution)/shard_map/ppermute | solution.py:72
  56.9 13.8 %collective-permute-start.19 = (bf16[80,1664]{1,0:T(8,128)(2,1)S(1)}, bf16[80,1664]{1,0:T(8,128)(2,1)S(1)}, u32[]{:S(2)}, u32[]{:S(2)}) collective-permute-start(bf16[80,1664]{1,0:T(8,128)(2,1)S(1)} %get-tuple-element.74), channel_id=1, source_target_pairs={{0,16},{8,24},{16,0},{24,8},{1,17},{9,25},{17,1},{25,9},{2,18},{10... | collective-permute-start | bytes 798728 | tf_op jit(solution)/shard_map/ppermute | solution.py:72
  57.7 13.1 %collective-permute-start.20 = (bf16[80,1664]{1,0:T(8,128)(2,1)S(1)}, bf16[80,1664]{1,0:T(8,128)(2,1)S(1)}, u32[]{:S(2)}, u32[]{:S(2)}) collective-permute-start(bf16[80,1664]{1,0:T(8,128)(2,1)S(1)} %get-tuple-element.75), channel_id=1, source_target_pairs={{0,24},{8,16},{16,8},{24,0},{1,25},{9,17},{17,9},{25,1},{2,26},{10... | collective-permute-start | bytes 798728 | tf_op jit(solution)/shard_map/ppermute | solution.py:72
  71.1 13.4 %collective-permute-start.21 = (bf16[24,1664]{1,0:T(8,128)(2,1)S(1)}, bf16[24,1664]{1,0:T(8,128)(2,1)S(1)}, u32[]{:S(2)}, u32[]{:S(2)}) collective-permute-start(bf16[24,1664]{1,0:T(8,128)(2,1)S(1)} %get-tuple-element.81), channel_id=1, source_target_pairs={{0,2},{2,0},{4,6},{6,4},{1,3},{3,1},{5,7},{7,5},{8,10},{10,8},{12,... | collective-permute-start | bytes 239624 | tf_op jit(solution)/shard_map/ppermute | solution.py:72
  73.5 11.0 %collective-permute-start.22 = (bf16[24,1664]{1,0:T(8,128)(2,1)S(1)}, bf16[24,1664]{1,0:T(8,128)(2,1)S(1)}, u32[]{:S(2)}, u32[]{:S(2)}) collective-permute-start(bf16[24,1664]{1,0:T(8,128)(2,1)S(1)} %get-tuple-element.82), channel_id=1, source_target_pairs={{0,4},{2,6},{4,0},{6,2},{1,5},{3,7},{5,1},{7,3},{8,12},{10,14},{12... | collective-permute-start | bytes 239624 | tf_op jit(solution)/shard_map/ppermute | solution.py:72
  75.2 9.4 %collective-permute-start.23 = (bf16[24,1664]{1,0:T(8,128)(2,1)S(1)}, bf16[24,1664]{1,0:T(8,128)(2,1)S(1)}, u32[]{:S(2)}, u32[]{:S(2)}) collective-permute-start(bf16[24,1664]{1,0:T(8,128)(2,1)S(1)} %get-tuple-element.83), channel_id=1, source_target_pairs={{0,6},{2,4},{4,2},{6,0},{1,7},{3,5},{5,3},{7,1},{8,14},{10,12},{12... | collective-permute-start | bytes 239624 | tf_op jit(solution)/shard_map/ppermute | solution.py:72
  (3 other events, 44.1 us)
where the time goes:
time: 85.8 us; the launch traced here: 85.6 us
  Pallas kernels  53.4 us (62%)
  starting transfers between devices  24.2 us (28%)
  waiting for transfers between devices  7.22 us (8%)
    pallas_call x12, Pallas kernels, call(): pl.pallas_call(body, in_specs=specs_in, out_specs=specs_out, out_shape=ou...  53.4 us
    ppermute x24, starting transfers between devices, move(): return lax.ppermute(value, axis, [(i, i ^ offset) for i in range(size)])  24.2 us
    ppermute x24, waiting for transfers between devices, move(): return lax.ppermute(value, axis, [(i, i ^ offset) for i in range(size)])  7.22 us
  transfers between devices with their start and end apart: 24, of which 6 were waited for; matrix products, arithmetic and copies ran while one was open for 0% of the time, Pallas kernels for 45%

commit v1 on v0

--- a/solution.py
+++ b/solution.py
@@ -179,6 +179,13 @@
     return (want == c).astype(f32).astype(bf16)
 
 
+def frame_moves(z, frames):
+    moved = []
+    for k in range(1, z.ex):
+        moved.append(move(frames[k], "ex", z.ex, k))
+    return [frames[0]] + moved
+
+
 def to_blocks(z, frames, after):
     def body(*refs):
         rows = dot(block_select(z), stack_frames(refs[: z.ex]))
@@ -190,8 +197,8 @@
     )
 
 
-def load_weights(weight, after):
-    n = weight.shape[0]
+def load_weights(weight, after, n):
+    dims = (n,) + weight.shape[1:]
 
     def body(w, _, out, mark, sem):
         copies = [pltpu.make_async_copy(w.at[e], out.at[e], sem.at[e]) for e in range(n)]
@@ -204,11 +211,11 @@
     return call(
         body,
         (weight, after),
-        [shape(weight.shape, weight.dtype), token()],
+        [shape(dims, weight.dtype), token()],
         [HBM, ANY],
         [VMEM, VMEM],
         [pltpu.SemaphoreType.DMA((n,))],
-        cost=2 * weight.size,
+        cost=2 * weight.size // weight.shape[0] * n,
     )
 
 
@@ -221,7 +228,8 @@
     mine = [mine[0]] + late
     others = []
     for c in range(1, z.dp):
-        others += [move(v, "dp", z.dp, c) for v in mine]
+        others.append(move(mine[0], "dp", z.dp, c))
+        others += [move(v, "dp", z.dp, c) for v in mine[1:]]
     return mine + others
 
 
@@ -236,7 +244,7 @@
         refs[i // z.et][i % z.et, pl.ds(start, z.rb), :] = value[i * z.rb : (i + 1) * z.rb]
 
 
-def per_expert(z, copy_ref, work):
+def per_expert(z, copy_ref, work, first=0, last=None):
     base = lax.axis_index("ex") * z.gs
 
     def step(e, carry):
@@ -252,7 +260,7 @@
 
         return carry
 
-    lax.fori_loop(0, z.gs, step, 0)
+    lax.fori_loop(first, z.gs if last is None else last, step, 0)
 
 
 def rows_of(ref, blocks):
@@ -292,16 +300,29 @@
     )
 
 
-def middle(z, copies, blocks, weight_in, weight_out, pre, hid):
+def middle(z, copies, blocks, weight_in, ready, weight_out, pre, hid, early):
+    done = ready.shape[0]
+
     def body(copy_ref, *refs):
         srcs = refs[: z.src]
-        win, wout, pre_ref, hid_ref, uall, slope, *outs = refs[z.src :]
+        win, wout, whbm, pre_ref, hid_ref, uall, slope, *outs = refs[z.src :]
+        *outs, grad, buf, sem, wrest, wsem = outs
+        fetch = [
+            pltpu.make_async_copy(whbm.at[e], wrest.at[e - done], wsem.at[e - done])
+            for e in range(done, z.gs)
+        ]
+        for c in fetch:
+            c.start()
         assemble(z, srcs, uall)
 
-        def work(e, ids):
-            back = dot_nt(rows_of(uall, ids), wout[e])
+        def write(e):
+            return pltpu.make_async_copy(buf, grad.at[e], sem)
+
+        def work(e, ids, last=False):
+            w = wrest[e - done] if last else wout[e]
+            back = dot_nt(rows_of(uall, ids), w)
             s = (back * gelu_slope(rows_of(pre_ref, ids))).astype(bf16)
-            o = dot(rows_of(hid_ref, ids), wout[e]).astype(bf16)
+            o = dot(rows_of(hid_ref, ids), w).astype(bf16)
             g = dot_nt(s, win[e]).astype(bf16)
             for i, b in enumerate(ids):
                 part = slice(i * z.rows, (i + 1) * z.rows)
@@ -309,30 +330,57 @@
                 scatter_rows(z, o[part], b, 0, outs)
                 scatter_rows(z, g[part], b, z.half, outs)
 
-        per_expert(z, copy_ref, work)
+        def early_work(e, ids):
+            work(e, ids)
+
+            @pl.when(e > 0)
+            def _():
+                write(e - 1).wait()
+
+            r = rows_of(uall, ids)
+            for i in range(z.f // 128):
+                part = slice(i * 128, (i + 1) * 128)
+                l = [hid_ref[b, :, part] for b in ids]
+                buf[part, :] = dot_tn(l[0] if len(ids) == 1 else jnp.concatenate(l, axis=0), r)
+            write(e).start()
+
+        per_expert(z, copy_ref, early_work, 0, early)
+        per_expert(z, copy_ref, work, early, done)
+        for c in fetch:
+            c.wait()
+        per_expert(z, copy_ref, lambda e, ids: work(e, ids, True), done, z.gs)
+        write(early - 1).wait()
 
     res = call(
         body,
-        (copies, *blocks, weight_in, weight_out, pre, hid),
+        (copies, *blocks, weight_in, ready, weight_out, pre, hid),
         [shape((z.nb, z.rows, z.d), bf16), shape((z.nb, z.rows, z.f), bf16)]
-        + [shape((z.et, 2 * z.half, z.d), bf16)] * z.dp,
-        [SMEM] + [VMEM] * (z.src + 4),
-        [VMEM] * (2 + z.dp),
+        + [shape((z.et, 2 * z.half, z.d), bf16)] * z.dp
+        + [pltpu.HBM((z.gs, z.f, z.d), f32)],
+        [SMEM] + [VMEM] * (z.src + 2) + [HBM, VMEM, VMEM],
+        [VMEM] * (2 + z.dp) + [HBM],
+        [
+            pltpu.VMEM((z.f, z.d), f32),
+            pltpu.SemaphoreType.DMA(()),
+            pltpu.VMEM((z.gs - done, z.f, z.d), bf16),
+            pltpu.SemaphoreType.DMA((z.gs - done,)),
+        ],
+        limit=15,
         cost=48 * 2**20,
     )
-    return res[0], res[1], res[2:]
+    return res[0], res[1], res[2:-1], res[-1]
 
 
 def weight_grads(z, copies, rows, jobs, held, after):
-    kinds = [which for which, _, _ in jobs]
+    jobs = [job for job in jobs if job[1] < job[2]]
+    kinds = sorted({job[0] for job in jobs})
     operands, spans, alias = [], [], {}
     for which in kinds:
         operands += list(rows[which])
     for which in kinds:
         tiles = rows[which][0].shape[2] // 128
-        edge = (tiles + 1) // 2 * 128
-        spans.append(((0, edge), (edge, tiles * 128 - edge)))
-    parts = 2
+        edges = [-(-tiles * p // 4) * 128 for p in range(5)]
+        spans.append([(a, b - a) for a, b in zip(edges, edges[1:])])
     old = [held[which] for which in kinds if held[which] is not None]
     at = 1 + len(operands)
     for i, which in enumerate(kinds):
@@ -343,50 +391,48 @@
     def body(copy_ref, *refs):
         ins = refs[: len(operands)]
         outs = refs[len(operands) + len(old) + 1 :]
-        mark = outs[len(jobs)]
+        mark = outs[len(kinds)]
+        bufs = outs[len(kinds) + 1 : -1]
         sems = outs[-1]
         mark[...] = jnp.zeros_like(mark)
-        base = lax.axis_index("ex") * z.gs
 
         def copy_of(i, e, p):
             start, size = spans[i][p]
-            src = outs[len(jobs) + 1 + i].at[pl.ds(start, size), :]
+            src = bufs[i].at[pl.ds(start, size), :]
             return pltpu.make_async_copy(src, outs[i].at[e, pl.ds(start, size), :], sems.at[i, p])
 
-        def work(i, first, e, ids):
-            left, right = ins[2 * i], ins[2 * i + 1]
-            buf = outs[len(jobs) + 1 + i]
-            r = rows_of(right, ids)
-            for p, (start, size) in enumerate(spans[i]):
+        def work(i, first, parts, busy, e, ids):
+            left = ins[2 * i]
+            r = rows_of(ins[2 * i + 1], ids)
+            for p in parts:
+                start, size = spans[i][p]
                 l = [left[b, :, start : start + size] for b in ids]
                 v = dot_tn(l[0] if len(ids) == 1 else jnp.concatenate(l, axis=0), r)
-
-                @pl.when(e > first)
-                def _():
+                if (i, p) in busy:
                     copy_of(i, e - 1, p).wait()
-
-                buf[start : start + size, :] = v
+                else:
+
+                    @pl.when(e > first)
+                    def _():
+                        copy_of(i, e - 1, p).wait()
+
+                bufs[i][start : start + size, :] = v
                 copy_of(i, e, p).start()
 
-        for i, (which, first, last) in enumerate(jobs):
-
-            def step(e, carry):
-                doubled = copy_ref[base + e] > 1
-
-                @pl.when(doubled)
-                def _():
-                    work(i, first, e, (e, z.gs))
-
-                @pl.when(jnp.logical_not(doubled))
-                def _():
-                    work(i, first, e, (e,))
-
-                return carry
-
-            lax.fori_loop(first, last, step, 0)
-        for i, (which, first, last) in enumerate(jobs):
-            for p in range(parts):
-                copy_of(i, last - 1, p).wait()
+        pending = {}
+        for which, first, last, parts in jobs:
+            i = kinds.index(which)
+            parts = [p for p in parts if spans[i][p][1] > 0]
+            busy = frozenset(pending)
+
+            def one(e, ids, i=i, first=first, parts=parts, busy=busy):
+                work(i, first, parts, busy, e, ids)
+
+            per_expert(z, copy_ref, one, first, last)
+            for p in parts:
+                pending[(i, p)] = last - 1
+        for (i, p), e in pending.items():
+            copy_of(i, e, p).wait()
 
     outs = [
         pltpu.HBM((z.gs, rows[which][0].shape[2], rows[which][1].shape[2]), f32)
@@ -397,11 +443,11 @@
         (copies, *operands, *old, after),
         outs + [token()],
         [SMEM] + [VMEM] * len(operands) + [HBM] * len(old) + [ANY],
-        [HBM] * len(jobs) + [VMEM],
+        [HBM] * len(kinds) + [VMEM],
         [pltpu.VMEM((rows[w][0].shape[2], rows[w][1].shape[2]), f32) for w in kinds]
-        + [pltpu.SemaphoreType.DMA((len(jobs), parts))],
+        + [pltpu.SemaphoreType.DMA((len(kinds), 4))],
         limit=24,
-        cost=4 * sum((last - first) * rows[w][0].shape[2] * rows[w][1].shape[2] for w, first, last in jobs),
+        cost=4 * z.f * z.d * sum(job[2] - job[1] for job in jobs),
         aliases=alias,
     )
     held = list(held)
@@ -472,26 +518,35 @@
     z = Sizes(tokens, weight_in, copies)
     gates = gate_probs.T
     frames, tables = send_frame(z, tokens, gates, expert_ids.T, copies, cotangent)
-    got = [frames[0]] + [move(frames[k], "ex", z.ex, k) for k in range(1, z.ex)]
-    win, mark = load_weights(weight_in, frames[0])
+    got = frame_moves(z, frames)
+    win, mark = load_weights(weight_in, frames[0], z.gs)
     own_x, own_u = to_blocks(z, got, mark)
     mine_x = plane_moves(z, own_x)
     mine_u = plane_moves(z, own_u)
-    wout, mark = load_weights(weight_out, own_x)
+    wout, mark = load_weights(weight_out, own_x, z.gs // 2)
     blocks_x = swap_cores(z, mine_x, mark)
     xall, pre, hid, mark = forward_in(z, copies, blocks_x, win, wout)
     blocks_u = swap_cores(z, mine_u, mark)
-    uall, slope, parts = middle(z, copies, blocks_u, win, wout, pre, hid)
+    early = 1
+    split = z.gs // 2
+    uall, slope, parts, grad_out = middle(
+        z, copies, blocks_u, win, wout, weight_out, pre, hid, early
+    )
     pairs = ((hid, uall), (xall, slope))
-    held = [None, None]
+    held = [grad_out, None]
     swapped = [move(parts[c], "dp", z.dp, c) for c in range(1, z.dp)]
-    held, mark = weight_grads(z, copies, pairs, [(0, 0, 1)], held, parts[1])
+    held, mark = weight_grads(z, copies, pairs, [(0, early, early + 1, (0, 1))], held, parts[1])
     sums = pair_sum(z, parts[0], swapped, mark)
     parts = [sums[0]] + [move(sums[m], "et", z.et, m) for m in range(1, z.et)]
-    held, mark = weight_grads(z, copies, pairs, [(0, 1, z.gs), (1, 0, 1)], held, sums[0])
+    jobs = [
+        (0, early, early + 1, (2, 3)),
+        (0, early + 1, z.gs, range(4)),
+        (1, 0, split, range(4)),
+    ]
+    held, mark = weight_grads(z, copies, pairs, jobs, held, sums[0])
     frames = to_frames(z, parts, mark)
-    frames = [frames[0]] + [move(frames[k], "ex", z.ex, k) for k in range(1, z.ex)]
-    held, mark = weight_grads(z, copies, pairs, [(1, 1, z.gs)], held, frames[0])
+    frames = frame_moves(z, frames)
+    held, mark = weight_grads(z, copies, pairs, [(1, split, z.gs, range(4))], held, frames[0])
     grad_weight_out, grad_weight_in = held
     layer_out, grad_tokens, grad_gates = combine(z, gates, cotangent, tables, frames, mark)
     return (layer_out, grad_tokens, grad_gates.T, grad_weight_in, grad_weight_out)

time: 85.8 us -> 81.1 us (0.945)
  Pallas kernels: 53.4 us -> 49.3 us
    pallas_call x12, Pallas kernels: 53.4 us -> 49.3 us  [call(): pl.pallas_call(body, in_specs=specs_in, out_specs=specs_out, out_shape=ou...]
  transfers between devices with their start and end apart: 24 -> 24, of which waited for: 6 -> 6; matrix products, arithmetic and copies ran while one was open for 0% -> 0% of each run, Pallas kernels for 45% -> 41%
where the time goes in v1:
time: 81.1 us; the launch traced here: 81 us
  Pallas kernels  49.3 us (61%)
  starting transfers between devices  24 us (30%)
  waiting for transfers between devices  6.74 us (8%)
  between operations  0.82 us (1%)
    pallas_call x12, Pallas kernels, call(): pl.pallas_call(body, in_specs=specs_in, out_specs=specs_out, out_shape=ou...  49.3 us
    ppermute x24, starting transfers between devices, move(): return lax.ppermute(value, axis, [(i, i ^ offset) for i in range(size)])  24 us
    ppermute x24, waiting for transfers between devices, move(): return lax.ppermute(value, axis, [(i, i ^ offset) for i in range(size)])  6.74 us
  transfers between devices with their start and end apart: 24, of which 6 were waited for; matrix products, arithmetic and copies ran while one was open for 0% of the time, Pallas kernels for 41%

profile of v1, /device:TPU:0, one launch (start us, length us, event | category | flops | bytes accessed | tf_op | source)
XLA Modules:
  0.0 81.0 jit_solution(14027628405402799442)
XLA Ops:
  0.6 1.6 %shard_map.110 = (bf16[24,1664]{1,0:T(8,128)(2,1)S(1)}, bf16[24,1664]{1,0:T(8,128)(2,1)S(1)}, bf16[24,1664]{1,0:T(8,128)(2,1)S(1)}, bf16[24,1664]{1,0:T(8,128)(2...) custom-call(bf16[32,1664]{1,0:T(8,128)(2,1)} %refs_0_.1, ...), custom_call_target="tpu_custom_call" | custom-call | bytes 1048576 | tf_op jit(solution)/shard_map/pallas_call | solution.py:46
  2.2 3.1 %collective-permute-start = (bf16[24,1664]{1,0:T(8,128)(2,1)S(1)}, bf16[24,1664]{1,0:T(8,128)(2,1)S(1)}, u32[]{:S(2)}, u32[]{:S(2)}) collective-permute-start(bf16[24,1664]{1,0:T(8,128)(2,1)S(1)} %get-tuple-element.53), channel_id=1, source_target_pairs={{0,2},{2,0},{4,6},{6,4},{1,3},{3,1},{5,7},{7,5},{8,10},{10,8},{12,... | collective-permute-start | bytes 239624 | tf_op jit(solution)/shard_map/ppermute | solution.py:72
  5.3 2.6 %collective-permute-start.1 = (bf16[24,1664]{1,0:T(8,128)(2,1)S(1)}, bf16[24,1664]{1,0:T(8,128)(2,1)S(1)}, u32[]{:S(2)}, u32[]{:S(2)}) collective-permute-start(bf16[24,1664]{1,0:T(8,128)(2,1)S(1)} %get-tuple-element.54), channel_id=1, source_target_pairs={{0,4},{2,6},{4,0},{6,2},{1,5},{3,7},{5,1},{7,3},{8,12},{10,14},{12... | collective-permute-start | bytes 239624 | tf_op jit(solution)/shard_map/ppermute | solution.py:72
  7.9 5.0 %shard_map.111 = (bf16[4,1664,1024]{2,1,0:T(8,128)(2,1)S(1)}, f32[8,128]{1,0:T(8,128)S(1)}) custom-call(bf16[4,1664,1024]{2,1,0:T(8,128)(2,1)} %w.2, bf16[24,1664]{1,0:T(8,128)(2,1)S(1)} %get-tuple-element.52._.refs_0_), custom_call_target="tpu_custom_call" | custom-call | bytes 13631488 | tf_op jit(solution)/shard_map/pallas_call | solution.py:46
  12.9 1.4 %collective-permute-done.1.refs_2_ = bf16[24,1664]{1,0:T(8,128)(2,1)S(1)} collective-permute-done((bf16[24,1664]{1,0:T(8,128)(2,1)S(1)}, bf16[24,1664]{1,0:T(8,128)(2,1)S(1)}, u32[]{:S(2)}, u32[]{:S(2)}) %collective-permute-start.1) | collective-permute-done | bytes 79904 | tf_op jit(solution)/shard_map/ppermute | solution.py:72
  14.6 2.5 %collective-permute-start.12 = (bf16[40,1664]{1,0:T(8,128)(2,1)S(1)}, bf16[40,1664]{1,0:T(8,128)(2,1)S(1)}, u32[]{:S(2)}, u32[]{:S(2)}) collective-permute-start(bf16[40,1664]{1,0:T(8,128)(2,1)S(1)} %get-tuple-element.62._.refs_0_), channel_id=1, source_target_pairs={{0,24},{8,16},{16,8},{24,0},{1,25},{9,17},{17,9},{25,1},{2,26},{10... | collective-permute-start | bytes 399368 | tf_op jit(solution)/shard_map/ppermute | solution.py:72
  18.1 2.5 %collective-permute-start.5 = (bf16[40,1664]{1,0:T(8,128)(2,1)S(1)}, bf16[40,1664]{1,0:T(8,128)(2,1)S(1)}, u32[]{:S(2)}, u32[]{:S(2)}) collective-permute-start(bf16[40,1664]{1,0:T(8,128)(2,1)S(1)} %get-tuple-element.57.refs_0_), channel_id=1, source_target_pairs={{0,24},{8,16},{16,8},{24,0},{1,25},{9,17},{17,9},{25,1},{2,26},{10... | collective-permute-start | bytes 399368 | tf_op jit(solution)/shard_map/ppermute | solution.py:72
  21.1 1.0 %collective-permute-done.12.refs_3_ = bf16[40,1664]{1,0:T(8,128)(2,1)S(1)} collective-permute-done((bf16[40,1664]{1,0:T(8,128)(2,1)S(1)}, bf16[40,1664]{1,0:T(8,128)(2,1)S(1)}, u32[]{:S(2)}, u32[]{:S(2)}) %collective-permute-start.12) | collective-permute-done | bytes 133152 | tf_op jit(solution)/shard_map/ppermute | solution.py:72
  22.1 1.4 %collective-permute-start.3 = (bf16[40,1664]{1,0:T(8,128)(2,1)S(1)}, bf16[40,1664]{1,0:T(8,128)(2,1)S(1)}, u32[]{:S(2)}, u32[]{:S(2)}) collective-permute-start(bf16[40,1664]{1,0:T(8,128)(2,1)S(1)} %get-tuple-element.57.refs_0_), channel_id=1, source_target_pairs={{0,8},{8,0},{16,24},{24,16},{1,9},{9,1},{17,25},{25,17},{2,10},{10... | collective-permute-start | bytes 399368 | tf_op jit(solution)/shard_map/ppermute | solution.py:72
  23.5 2.0 %collective-permute-done.11.refs_2_ = bf16[40,1664]{1,0:T(8,128)(2,1)S(1)} collective-permute-done((bf16[40,1664]{1,0:T(8,128)(2,1)S(1)}, bf16[40,1664]{1,0:T(8,128)(2,1)S(1)}, u32[]{:S(2)}, u32[]{:S(2)}) %collective-permute-start.11) | collective-permute-done | bytes 133152 | tf_op jit(solution)/shard_map/ppermute | solution.py:72
  26.1 1.2 %collective-permute-done.5.refs_3_ = bf16[40,1664]{1,0:T(8,128)(2,1)S(1)} collective-permute-done((bf16[40,1664]{1,0:T(8,128)(2,1)S(1)}, bf16[40,1664]{1,0:T(8,128)(2,1)S(1)}, u32[]{:S(2)}, u32[]{:S(2)}) %collective-permute-start.5) | collective-permute-done | bytes 133152 | tf_op jit(solution)/shard_map/ppermute | solution.py:72
  27.2 0.9 %collective-permute-done.4.refs_2_ = bf16[40,1664]{1,0:T(8,128)(2,1)S(1)} collective-permute-done((bf16[40,1664]{1,0:T(8,128)(2,1)S(1)}, bf16[40,1664]{1,0:T(8,128)(2,1)S(1)}, u32[]{:S(2)}, u32[]{:S(2)}) %collective-permute-start.4) | collective-permute-done | bytes 133152 | tf_op jit(solution)/shard_map/ppermute | solution.py:72
  29.2 3.6 %shard_map.113 = (bf16[2,1024,1664]{2,1,0:T(8,128)(2,1)S(1)}, f32[8,128]{1,0:T(8,128)}) custom-call(bf16[4,1024,1664]{2,1,0:T(8,128)(2,1)} %refs_10_.1, bf16[40,1664]{1,0:T(8,128)(2,1)S(1)} %get-tuple-element.62._.refs_0_), custom_call_target="tpu_custom_call" | custom-call | bytes 6815744 | tf_op jit(solution)/shard_map/pallas_call | solution.py:46
  32.9 4.4 %shard_map.114 = (bf16[5,64,1664]{2,1,0:T(8,128)(2,1)S(1)}, f32[5,64,1024]{2,1,0:T(8,128)S(1)}, bf16[5,64,1024]{2,1,0:T(8,128)(2,1)S(1)}, f32[8,128]{1,0:T(8,128)}) custom-call(s32[16]{0:T(128)S(1)} %copy-done.1, bf16[40,1664]{1,0:T(8,128)(2,1)S(1)} %get-tuple-element.62._.refs_0_, bf16[40,1664]{1,0:T(8,128)(2,1)S(1)} %collective-permute-done.10.refs_1_, ...), custom_call_target="tpu_custom_call" | custom-call | bytes 16777216 | tf_op jit(solution)/shard_map/pallas_call | solution.py:46
  37.3 13.0 %shard_map.115 = (bf16[5,64,1664]{2,1,0:T(8,128)(2,1)S(1)}, bf16[5,64,1024]{2,1,0:T(8,128)(2,1)S(1)}, bf16[4,80,1664]{2,1,0:T(8,128)(2,1)S(1)}, bf16[4,80,1664]{2,1,0:T(8,128)(2,1)S(1)}, f32[4,1024,1664]{2,1,0:T(8,128)}) custom-call(s32[16]{0:T(128)S(1)} %copy-done.1, bf16[40,1664]{1,0:T(8,128)(2,1)S(1)} %get-tuple-element.57.refs_0_, ...), custom_call_target="tpu_custom_call" | custom-call | bytes 50331648 | tf_op jit(solution)/shard_map/pallas_call | solution.py:46
  50.8 2.8 %shard_map.116 = (f32[4,1024,1664]{2,1,0:T(8,128)}, f32[8,128]{1,0:T(8,128)S(1)}) custom-call(s32[16]{0:T(128)S(1)} %copy-done.1, bf16[5,64,1024]{2,1,0:T(8,128)(2,1)S(1)} %get-tuple-element.68.refs_12_.refs_0_, bf16[5,64,1664]{2,1,0:T(8,128)(2,1)S(1)} %get-tuple-element.71.refs_1_, ...), custom_call_target="tpu_custom_call", output_to_operand_aliasing={{0}: (3, {})} | custom-call | bytes 6815744 | tf_op jit(solution)/shard_map/pallas_call | solution.py:46
  53.9 1.0 %collective-permute-start.18 = (bf16[80,1664]{1,0:T(8,128)(2,1)S(1)}, bf16[80,1664]{1,0:T(8,128)(2,1)S(1)}, u32[]{:S(2)}, u32[]{:S(2)}) collective-permute-start(bf16[80,1664]{1,0:T(8,128)(2,1)S(1)} %get-tuple-element.75), channel_id=1, source_target_pairs={{0,8},{8,0},{16,24},{24,16},{1,9},{9,1},{17,25},{25,17},{2,10},{10... | collective-permute-start | bytes 798728 | tf_op jit(solution)/shard_map/ppermute | solution.py:72
  55.6 1.8 %collective-permute-start.20 = (bf16[80,1664]{1,0:T(8,128)(2,1)S(1)}, bf16[80,1664]{1,0:T(8,128)(2,1)S(1)}, u32[]{:S(2)}, u32[]{:S(2)}) collective-permute-start(bf16[80,1664]{1,0:T(8,128)(2,1)S(1)} %get-tuple-element.77), channel_id=1, source_target_pairs={{0,24},{8,16},{16,8},{24,0},{1,25},{9,17},{17,9},{25,1},{2,26},{10... | collective-permute-start | bytes 798728 | tf_op jit(solution)/shard_map/ppermute | solution.py:72
  57.4 11.1 %shard_map.118 = (f32[4,1024,1664]{2,1,0:T(8,128)}, f32[4,1664,1024]{2,1,0:T(8,128)}, f32[8,128]{1,0:T(8,128)S(1)}) custom-call(s32[16]{0:T(128)S(1)} %copy-done.1, bf16[5,64,1024]{2,1,0:T(8,128)(2,1)S(1)} %get-tuple-element.68.refs_12_.refs_0_, bf16[5,64,1664]{2,1,0:T(8,128)(2,1)S(1)} %get-tuple-element.71.refs_1_, ...), custom_call_target="tpu_custom_call", output_to_operand_aliasing={{0}: (5, {})} | custom-call | bytes 34078720 | tf_op jit(solution)/shard_map/pallas_call | solution.py:46
  69.0 2.3 %collective-permute-start.21 = (bf16[24,1664]{1,0:T(8,128)(2,1)S(1)}, bf16[24,1664]{1,0:T(8,128)(2,1)S(1)}, u32[]{:S(2)}, u32[]{:S(2)}) collective-permute-start(bf16[24,1664]{1,0:T(8,128)(2,1)S(1)} %get-tuple-element.83), channel_id=1, source_target_pairs={{0,2},{2,0},{4,6},{6,4},{1,3},{3,1},{5,7},{7,5},{8,10},{10,8},{12,... | collective-permute-start | bytes 239624 | tf_op jit(solution)/shard_map/ppermute | solution.py:72
  71.3 1.6 %collective-permute-start.22 = (bf16[24,1664]{1,0:T(8,128)(2,1)S(1)}, bf16[24,1664]{1,0:T(8,128)(2,1)S(1)}, u32[]{:S(2)}, u32[]{:S(2)}) collective-permute-start(bf16[24,1664]{1,0:T(8,128)(2,1)S(1)} %get-tuple-element.84), channel_id=1, source_target_pairs={{0,4},{2,6},{4,0},{6,2},{1,5},{3,7},{5,1},{7,3},{8,12},{10,14},{12... | collective-permute-start | bytes 239624 | tf_op jit(solution)/shard_map/ppermute | solution.py:72
  73.0 0.8 collective-permute-start.23
  73.8 6.1 %shard_map.120 = (f32[4,1664,1024]{2,1,0:T(8,128)}, f32[8,128]{1,0:T(8,128)S(1)}) custom-call(s32[16]{0:T(128)S(1)} %copy-done.1, bf16[5,64,1664]{2,1,0:T(8,128)(2,1)S(1)} %get-tuple-element.78.refs_2_.refs_0_, bf16[5,64,1024]{2,1,0:T(8,128)(2,1)S(1)} %get-tuple-element.79.refs_3_.refs_1_, ...), custom_call_target="tpu_custom_call", output_to_operand_aliasing={{0}: (3, {})} | custom-call | bytes 13631488 | tf_op jit(solution)/shard_map/pallas_call | solution.py:46
  80.0 1.0 %shard_map.121 = (bf16[32,1664]{1,0:T(8,128)(2,1)}, bf16[32,1664]{1,0:T(8,128)(2,1)}, f32[2,32]{1,0:T(2,128)}) custom-call(f32[2,32]{1,0:T(2,128)S(1)} %bitcast.6, bf16[32,1664]{1,0:T(8,128)(2,1)S(1)} %copy-done, bf16[96,32]{1,0:T(8,128)(2,1)S(1)} %get-tuple-element.49.t0, bf16[96,32]{1,0:T(8,128)(2,1)S(1)} %get-tuple-element.50.t1, ...), custom_call_target="tpu_custom_call" | custom-call | bytes 1048576 | tf_op jit(solution)/shard_map/pallas_call | solution.py:46
  (42 shorter events, 5.4 us)
Async XLA Ops:
  2.2 10.7 %collective-permute-start = (bf16[24,1664]{1,0:T(8,128)(2,1)S(1)}, bf16[24,1664]{1,0:T(8,128)(2,1)S(1)}, u32[]{:S(2)}, u32[]{:S(2)}) collective-permute-start(bf16[24,1664]{1,0:T(8,128)(2,1)S(1)} %get-tuple-element.53), channel_id=1, source_target_pairs={{0,2},{2,0},{4,6},{6,4},{1,3},{3,1},{5,7},{7,5},{8,10},{10,8},{12,... | collective-permute-start | bytes 239624 | tf_op jit(solution)/shard_map/ppermute | solution.py:72
  5.3 9.0 %collective-permute-start.1 = (bf16[24,1664]{1,0:T(8,128)(2,1)S(1)}, bf16[24,1664]{1,0:T(8,128)(2,1)S(1)}, u32[]{:S(2)}, u32[]{:S(2)}) collective-permute-start(bf16[24,1664]{1,0:T(8,128)(2,1)S(1)} %get-tuple-element.54), channel_id=1, source_target_pairs={{0,4},{2,6},{4,0},{6,2},{1,5},{3,7},{5,1},{7,3},{8,12},{10,14},{12... | collective-permute-start | bytes 239624 | tf_op jit(solution)/shard_map/ppermute | solution.py:72
  7.9 6.5 %collective-permute-start.2 = (bf16[24,1664]{1,0:T(8,128)(2,1)S(1)}, bf16[24,1664]{1,0:T(8,128)(2,1)S(1)}, u32[]{:S(2)}, u32[]{:S(2)}) collective-permute-start(bf16[24,1664]{1,0:T(8,128)(2,1)S(1)} %get-tuple-element.55), channel_id=1, source_target_pairs={{0,6},{2,4},{4,2},{6,0},{1,7},{3,5},{5,3},{7,1},{8,14},{10,12},{12... | collective-permute-start | bytes 239624 | tf_op jit(solution)/shard_map/ppermute | solution.py:72
  14.6 7.5 %collective-permute-start.12 = (bf16[40,1664]{1,0:T(8,128)(2,1)S(1)}, bf16[40,1664]{1,0:T(8,128)(2,1)S(1)}, u32[]{:S(2)}, u32[]{:S(2)}) collective-permute-start(bf16[40,1664]{1,0:T(8,128)(2,1)S(1)} %get-tuple-element.62._.refs_0_), channel_id=1, source_target_pairs={{0,24},{8,16},{16,8},{24,0},{1,25},{9,17},{17,9},{25,1},{2,26},{10... | collective-permute-start | bytes 399368 | tf_op jit(solution)/shard_map/ppermute | solution.py:72
  17.1 8.4 %collective-permute-start.11 = (bf16[40,1664]{1,0:T(8,128)(2,1)S(1)}, bf16[40,1664]{1,0:T(8,128)(2,1)S(1)}, u32[]{:S(2)}, u32[]{:S(2)}) collective-permute-start(bf16[40,1664]{1,0:T(8,128)(2,1)S(1)} %get-tuple-element.62._.refs_0_), channel_id=1, source_target_pairs={{0,16},{8,24},{16,0},{24,8},{1,17},{9,25},{17,1},{25,9},{2,18},{10... | collective-permute-start | bytes 399368 | tf_op jit(solution)/shard_map/ppermute | solution.py:72
  17.6 7.9 %collective-permute-start.10 = (bf16[40,1664]{1,0:T(8,128)(2,1)S(1)}, bf16[40,1664]{1,0:T(8,128)(2,1)S(1)}, u32[]{:S(2)}, u32[]{:S(2)}) collective-permute-start(bf16[40,1664]{1,0:T(8,128)(2,1)S(1)} %get-tuple-element.62._.refs_0_), channel_id=1, source_target_pairs={{0,8},{8,0},{16,24},{24,16},{1,9},{9,1},{17,25},{25,17},{2,10},{10... | collective-permute-start | bytes 399368 | tf_op jit(solution)/shard_map/ppermute | solution.py:72
  18.1 9.1 %collective-permute-start.5 = (bf16[40,1664]{1,0:T(8,128)(2,1)S(1)}, bf16[40,1664]{1,0:T(8,128)(2,1)S(1)}, u32[]{:S(2)}, u32[]{:S(2)}) collective-permute-start(bf16[40,1664]{1,0:T(8,128)(2,1)S(1)} %get-tuple-element.57.refs_0_), channel_id=1, source_target_pairs={{0,24},{8,16},{16,8},{24,0},{1,25},{9,17},{17,9},{25,1},{2,26},{10... | collective-permute-start | bytes 399368 | tf_op jit(solution)/shard_map/ppermute | solution.py:72
  20.6 7.5 %collective-permute-start.4 = (bf16[40,1664]{1,0:T(8,128)(2,1)S(1)}, bf16[40,1664]{1,0:T(8,128)(2,1)S(1)}, u32[]{:S(2)}, u32[]{:S(2)}) collective-permute-start(bf16[40,1664]{1,0:T(8,128)(2,1)S(1)} %get-tuple-element.57.refs_0_), channel_id=1, source_target_pairs={{0,16},{8,24},{16,0},{24,8},{1,17},{9,25},{17,1},{25,9},{2,18},{10... | collective-permute-start | bytes 399368 | tf_op jit(solution)/shard_map/ppermute | solution.py:72
  22.1 6.1 %collective-permute-start.3 = (bf16[40,1664]{1,0:T(8,128)(2,1)S(1)}, bf16[40,1664]{1,0:T(8,128)(2,1)S(1)}, u32[]{:S(2)}, u32[]{:S(2)}) collective-permute-start(bf16[40,1664]{1,0:T(8,128)(2,1)S(1)} %get-tuple-element.57.refs_0_), channel_id=1, source_target_pairs={{0,8},{8,0},{16,24},{24,16},{1,9},{9,1},{17,25},{25,17},{2,10},{10... | collective-permute-start | bytes 399368 | tf_op jit(solution)/shard_map/ppermute | solution.py:72
  25.5 3.1 %collective-permute-start.13 = (bf16[40,1664]{1,0:T(8,128)(2,1)S(1)}, bf16[40,1664]{1,0:T(8,128)(2,1)S(1)}, u32[]{:S(2)}, u32[]{:S(2)}) collective-permute-start(bf16[40,1664]{1,0:T(8,128)(2,1)S(1)} %get-tuple-element.62._.refs_0_), channel_id=1, source_target_pairs={{0,1},{1,0},{2,3},{3,2},{4,5},{5,4},{6,7},{7,6},{8,9},{9,8},{10,11... | collective-permute-start | bytes 399368 | tf_op jit(solution)/shard_map/ppermute | solution.py:72
  25.5 3.2 %collective-permute-start.14 = (bf16[40,1664]{1,0:T(8,128)(2,1)S(1)}, bf16[40,1664]{1,0:T(8,128)(2,1)S(1)}, u32[]{:S(2)}, u32[]{:S(2)}) collective-permute-start(bf16[40,1664]{1,0:T(8,128)(2,1)S(1)} %collective-permute-done.10.refs_1_), channel_id=1, source_target_pairs={{0,1},{1,0},{2,3},{3,2},{4,5},{5,4},{6,7},{7,6},{8,9},{9,8},{10,11... | collective-permute-start | bytes 399368 | tf_op jit(solution)/shard_map/ppermute | solution.py:72
  27.2 1.9 %collective-permute-start.15 = (bf16[40,1664]{1,0:T(8,128)(2,1)S(1)}, bf16[40,1664]{1,0:T(8,128)(2,1)S(1)}, u32[]{:S(2)}, u32[]{:S(2)}) collective-permute-start(bf16[40,1664]{1,0:T(8,128)(2,1)S(1)} %collective-permute-done.11.refs_2_), channel_id=1, source_target_pairs={{0,1},{1,0},{2,3},{3,2},{4,5},{5,4},{6,7},{7,6},{8,9},{9,8},{10,11... | collective-permute-start | bytes 399368 | tf_op jit(solution)/shard_map/ppermute | solution.py:72
  28.1 9.2 %collective-permute-start.6 = (bf16[40,1664]{1,0:T(8,128)(2,1)S(1)}, bf16[40,1664]{1,0:T(8,128)(2,1)S(1)}, u32[]{:S(2)}, u32[]{:S(2)}) collective-permute-start(bf16[40,1664]{1,0:T(8,128)(2,1)S(1)} %get-tuple-element.57.refs_0_), channel_id=1, source_target_pairs={{0,1},{1,0},{2,3},{3,2},{4,5},{5,4},{6,7},{7,6},{8,9},{9,8},{10,11... | collective-permute-start | bytes 399368 | tf_op jit(solution)/shard_map/ppermute | solution.py:72
  28.1 4.7 %collective-permute-start.16 = (bf16[40,1664]{1,0:T(8,128)(2,1)S(1)}, bf16[40,1664]{1,0:T(8,128)(2,1)S(1)}, u32[]{:S(2)}, u32[]{:S(2)}) collective-permute-start(bf16[40,1664]{1,0:T(8,128)(2,1)S(1)} %collective-permute-done.12.refs_3_), channel_id=1, source_target_pairs={{0,1},{1,0},{2,3},{3,2},{4,5},{5,4},{6,7},{7,6},{8,9},{9,8},{10,11... | collective-permute-start | bytes 399368 | tf_op jit(solution)/shard_map/ppermute | solution.py:72
  28.6 8.6 %collective-permute-start.7 = (bf16[40,1664]{1,0:T(8,128)(2,1)S(1)}, bf16[40,1664]{1,0:T(8,128)(2,1)S(1)}, u32[]{:S(2)}, u32[]{:S(2)}) collective-permute-start(bf16[40,1664]{1,0:T(8,128)(2,1)S(1)} %collective-permute-done.3.refs_1_), channel_id=1, source_target_pairs={{0,1},{1,0},{2,3},{3,2},{4,5},{5,4},{6,7},{7,6},{8,9},{9,8},{10,11... | collective-permute-start | bytes 399368 | tf_op jit(solution)/shard_map/ppermute | solution.py:72
  28.7 8.6 %collective-permute-start.8 = (bf16[40,1664]{1,0:T(8,128)(2,1)S(1)}, bf16[40,1664]{1,0:T(8,128)(2,1)S(1)}, u32[]{:S(2)}, u32[]{:S(2)}) collective-permute-start(bf16[40,1664]{1,0:T(8,128)(2,1)S(1)} %collective-permute-done.4.refs_2_), channel_id=1, source_target_pairs={{0,1},{1,0},{2,3},{3,2},{4,5},{5,4},{6,7},{7,6},{8,9},{9,8},{10,11... | collective-permute-start | bytes 399368 | tf_op jit(solution)/shard_map/ppermute | solution.py:72
  29.1 8.1 %collective-permute-start.9 = (bf16[40,1664]{1,0:T(8,128)(2,1)S(1)}, bf16[40,1664]{1,0:T(8,128)(2,1)S(1)}, u32[]{:S(2)}, u32[]{:S(2)}) collective-permute-start(bf16[40,1664]{1,0:T(8,128)(2,1)S(1)} %collective-permute-done.5.refs_3_), channel_id=1, source_target_pairs={{0,1},{1,0},{2,3},{3,2},{4,5},{5,4},{6,7},{7,6},{8,9},{9,8},{10,11... | collective-permute-start | bytes 399368 | tf_op jit(solution)/shard_map/ppermute | solution.py:72
  50.3 3.3 %collective-permute-start.17 = (bf16[4,80,1664]{2,1,0:T(8,128)(2,1)S(1)}, bf16[4,80,1664]{2,1,0:T(8,128)(2,1)S(1)}, u32[]{:S(2)}, u32[]{:S(2)}) collective-permute-start(bf16[4,80,1664]{2,1,0:T(8,128)(2,1)S(1)} %get-tuple-element.70.refs_3_), channel_id=1, source_target_pairs={{0,1},{1,0},{2,3},{3,2},{4,5},{5,4},{6,7},{7,6},{8,9},{9,8},{10,11... | collective-permute-start | bytes 3194888 | tf_op jit(solution)/shard_map/ppermute | solution.py:72
  53.9 14.6 %collective-permute-start.18 = (bf16[80,1664]{1,0:T(8,128)(2,1)S(1)}, bf16[80,1664]{1,0:T(8,128)(2,1)S(1)}, u32[]{:S(2)}, u32[]{:S(2)}) collective-permute-start(bf16[80,1664]{1,0:T(8,128)(2,1)S(1)} %get-tuple-element.75), channel_id=1, source_target_pairs={{0,8},{8,0},{16,24},{24,16},{1,9},{9,1},{17,25},{25,17},{2,10},{10... | collective-permute-start | bytes 798728 | tf_op jit(solution)/shard_map/ppermute | solution.py:72
  54.9 13.8 %collective-permute-start.19 = (bf16[80,1664]{1,0:T(8,128)(2,1)S(1)}, bf16[80,1664]{1,0:T(8,128)(2,1)S(1)}, u32[]{:S(2)}, u32[]{:S(2)}) collective-permute-start(bf16[80,1664]{1,0:T(8,128)(2,1)S(1)} %get-tuple-element.76), channel_id=1, source_target_pairs={{0,16},{8,24},{16,0},{24,8},{1,17},{9,25},{17,1},{25,9},{2,18},{10... | collective-permute-start | bytes 798728 | tf_op jit(solution)/shard_map/ppermute | solution.py:72
  55.6 13.1 %collective-permute-start.20 = (bf16[80,1664]{1,0:T(8,128)(2,1)S(1)}, bf16[80,1664]{1,0:T(8,128)(2,1)S(1)}, u32[]{:S(2)}, u32[]{:S(2)}) collective-permute-start(bf16[80,1664]{1,0:T(8,128)(2,1)S(1)} %get-tuple-element.77), channel_id=1, source_target_pairs={{0,24},{8,16},{16,8},{24,0},{1,25},{9,17},{17,9},{25,1},{2,26},{10... | collective-permute-start | bytes 798728 | tf_op jit(solution)/shard_map/ppermute | solution.py:72
  69.0 10.9 %collective-permute-start.21 = (bf16[24,1664]{1,0:T(8,128)(2,1)S(1)}, bf16[24,1664]{1,0:T(8,128)(2,1)S(1)}, u32[]{:S(2)}, u32[]{:S(2)}) collective-permute-start(bf16[24,1664]{1,0:T(8,128)(2,1)S(1)} %get-tuple-element.83), channel_id=1, source_target_pairs={{0,2},{2,0},{4,6},{6,4},{1,3},{3,1},{5,7},{7,5},{8,10},{10,8},{12,... | collective-permute-start | bytes 239624 | tf_op jit(solution)/shard_map/ppermute | solution.py:72
  71.3 8.6 %collective-permute-start.22 = (bf16[24,1664]{1,0:T(8,128)(2,1)S(1)}, bf16[24,1664]{1,0:T(8,128)(2,1)S(1)}, u32[]{:S(2)}, u32[]{:S(2)}) collective-permute-start(bf16[24,1664]{1,0:T(8,128)(2,1)S(1)} %get-tuple-element.84), channel_id=1, source_target_pairs={{0,4},{2,6},{4,0},{6,2},{1,5},{3,7},{5,1},{7,3},{8,12},{10,14},{12... | collective-permute-start | bytes 239624 | tf_op jit(solution)/shard_map/ppermute | solution.py:72
  73.0 6.9 %collective-permute-start.23 = (bf16[24,1664]{1,0:T(8,128)(2,1)S(1)}, bf16[24,1664]{1,0:T(8,128)(2,1)S(1)}, u32[]{:S(2)}, u32[]{:S(2)}) collective-permute-start(bf16[24,1664]{1,0:T(8,128)(2,1)S(1)} %get-tuple-element.85), channel_id=1, source_target_pairs={{0,6},{2,4},{4,2},{6,0},{1,7},{3,5},{5,3},{7,1},{8,14},{10,12},{12... | collective-permute-start | bytes 239624 | tf_op jit(solution)/shard_map/ppermute | solution.py:72
  (3 other events, 37.2 us)

commit v2 on v1

--- a/solution.py
+++ b/solution.py
@@ -300,12 +300,31 @@
     )
 
 
-def middle(z, copies, blocks, weight_in, ready, weight_out, pre, hid, early):
+def early_out(z, copies, ready, hid):
+    def body(copy_ref, w, hid_ref, out):
+        def work(e, ids):
+            o = dot(rows_of(hid_ref, ids), w[e]).astype(bf16)
+            for i, b in enumerate(ids):
+                out[b] = o[i * z.rows : (i + 1) * z.rows]
+
+        per_expert(z, copy_ref, work, 0, ready.shape[0])
+
+    return call(
+        body,
+        (copies, ready, hid),
+        shape((z.nb, z.rows, z.d), bf16),
+        [SMEM, VMEM, VMEM],
+        VMEM,
+        cost=8 * 2**20,
+    )
+
+
+def middle(z, copies, blocks, weight_in, ready, weight_out, pre, hid, made, early):
     done = ready.shape[0]
 
     def body(copy_ref, *refs):
         srcs = refs[: z.src]
-        win, wout, whbm, pre_ref, hid_ref, uall, slope, *outs = refs[z.src :]
+        win, wout, whbm, pre_ref, hid_ref, made_ref, uall, slope, *outs = refs[z.src :]
         *outs, grad, buf, sem, wrest, wsem = outs
         fetch = [
             pltpu.make_async_copy(whbm.at[e], wrest.at[e - done], wsem.at[e - done])
@@ -322,7 +341,10 @@
             w = wrest[e - done] if last else wout[e]
             back = dot_nt(rows_of(uall, ids), w)
             s = (back * gelu_slope(rows_of(pre_ref, ids))).astype(bf16)
-            o = dot(rows_of(hid_ref, ids), w).astype(bf16)
+            if last:
+                o = dot(rows_of(hid_ref, ids), w).astype(bf16)
+            else:
+                o = rows_of(made_ref, ids)
             g = dot_nt(s, win[e]).astype(bf16)
             for i, b in enumerate(ids):
                 part = slice(i * z.rows, (i + 1) * z.rows)
@@ -353,11 +375,11 @@
 
     res = call(
         body,
-        (copies, *blocks, weight_in, ready, weight_out, pre, hid),
+        (copies, *blocks, weight_in, ready, weight_out, pre, hid, made),
         [shape((z.nb, z.rows, z.d), bf16), shape((z.nb, z.rows, z.f), bf16)]
         + [shape((z.et, 2 * z.half, z.d), bf16)] * z.dp
         + [pltpu.HBM((z.gs, z.f, z.d), f32)],
-        [SMEM] + [VMEM] * (z.src + 2) + [HBM, VMEM, VMEM],
+        [SMEM] + [VMEM] * (z.src + 2) + [HBM, VMEM, VMEM, VMEM],
         [VMEM] * (2 + z.dp) + [HBM],
         [
             pltpu.VMEM((z.f, z.d), f32),
@@ -527,17 +549,20 @@
     blocks_x = swap_cores(z, mine_x, mark)
     xall, pre, hid, mark = forward_in(z, copies, blocks_x, win, wout)
     blocks_u = swap_cores(z, mine_u, mark)
+    made = early_out(z, copies, wout, hid)
     early = 1
     split = z.gs // 2
     uall, slope, parts, grad_out = middle(
-        z, copies, blocks_u, win, wout, weight_out, pre, hid, early
+        z, copies, blocks_u, win, wout, weight_out, pre, hid, made, early
     )
     pairs = ((hid, uall), (xall, slope))
     held = [grad_out, None]
     swapped = [move(parts[c], "dp", z.dp, c) for c in range(1, z.dp)]
     held, mark = weight_grads(z, copies, pairs, [(0, early, early + 1, (0, 1))], held, parts[1])
     sums = pair_sum(z, parts[0], swapped, mark)
-    parts = [sums[0]] + [move(sums[m], "et", z.et, m) for m in range(1, z.et)]
+    parts = [sums[0]]
+    for m in range(1, z.et):
+        parts.append(move(sums[m], "et", z.et, m))
     jobs = [
         (0, early, early + 1, (2, 3)),
         (0, early + 1, z.gs, range(4)),

time: 81.1 us -> 82 us (1.011)
    pallas_call x12 -> x13, Pallas kernels: 49.3 us -> 50.1 us  [call(): pl.pallas_call(body, in_specs=specs_in, out_specs=specs_out, out_shape=ou...]
  transfers between devices with their start and end apart: 24 -> 24, of which waited for: 6 -> 6; matrix products, arithmetic and copies ran while one was open for 0% -> 0% of each run, Pallas kernels for 41% -> 43%
where the time goes in v2:
time: 82 us; the launch traced here: 81.8 us
  Pallas kernels  50.1 us (61%)
  starting transfers between devices  24.1 us (29%)
  waiting for transfers between devices  6.74 us (8%)
  between operations  0.85 us (1%)
    pallas_call x13, Pallas kernels, call(): pl.pallas_call(body, in_specs=specs_in, out_specs=specs_out, out_shape=ou...  50.1 us
    ppermute x24, starting transfers between devices, move(): return lax.ppermute(value, axis, [(i, i ^ offset) for i in range(size)])  24.1 us
    ppermute x24, waiting for transfers between devices, move(): return lax.ppermute(value, axis, [(i, i ^ offset) for i in range(size)])  6.74 us
  transfers between devices with their start and end apart: 24, of which 6 were waited for; matrix products, arithmetic and copies ran while one was open for 0% of the time, Pallas kernels for 43%

profile of v2, /device:TPU:0, one launch (start us, length us, event | category | flops | bytes accessed | tf_op | source)
XLA Modules:
  0.0 81.8 jit_solution(5965542441542607514)
XLA Ops:
  0.6 1.6 %shard_map.110 = (bf16[24,1664]{1,0:T(8,128)(2,1)S(1)}, bf16[24,1664]{1,0:T(8,128)(2,1)S(1)}, bf16[24,1664]{1,0:T(8,128)(2,1)S(1)}, bf16[24,1664]{1,0:T(8,128)(2...) custom-call(bf16[32,1664]{1,0:T(8,128)(2,1)} %refs_0_.1, ...), custom_call_target="tpu_custom_call" | custom-call | bytes 1048576 | tf_op jit(solution)/shard_map/pallas_call | solution.py:46
  2.2 3.1 %collective-permute-start = (bf16[24,1664]{1,0:T(8,128)(2,1)S(1)}, bf16[24,1664]{1,0:T(8,128)(2,1)S(1)}, u32[]{:S(2)}, u32[]{:S(2)}) collective-permute-start(bf16[24,1664]{1,0:T(8,128)(2,1)S(1)} %get-tuple-element.53), channel_id=1, source_target_pairs={{0,2},{2,0},{4,6},{6,4},{1,3},{3,1},{5,7},{7,5},{8,10},{10,8},{12,... | collective-permute-start | bytes 239624 | tf_op jit(solution)/shard_map/ppermute | solution.py:72
  5.3 2.6 %collective-permute-start.1 = (bf16[24,1664]{1,0:T(8,128)(2,1)S(1)}, bf16[24,1664]{1,0:T(8,128)(2,1)S(1)}, u32[]{:S(2)}, u32[]{:S(2)}) collective-permute-start(bf16[24,1664]{1,0:T(8,128)(2,1)S(1)} %get-tuple-element.54), channel_id=1, source_target_pairs={{0,4},{2,6},{4,0},{6,2},{1,5},{3,7},{5,1},{7,3},{8,12},{10,14},{12... | collective-permute-start | bytes 239624 | tf_op jit(solution)/shard_map/ppermute | solution.py:72
  7.9 5.0 %shard_map.111 = (bf16[4,1664,1024]{2,1,0:T(8,128)(2,1)S(1)}, f32[8,128]{1,0:T(8,128)S(1)}) custom-call(bf16[4,1664,1024]{2,1,0:T(8,128)(2,1)} %w.2, bf16[24,1664]{1,0:T(8,128)(2,1)S(1)} %get-tuple-element.52._.refs_0_), custom_call_target="tpu_custom_call" | custom-call | bytes 13631488 | tf_op jit(solution)/shard_map/pallas_call | solution.py:46
  12.9 1.4 %collective-permute-done.1.refs_2_ = bf16[24,1664]{1,0:T(8,128)(2,1)S(1)} collective-permute-done((bf16[24,1664]{1,0:T(8,128)(2,1)S(1)}, bf16[24,1664]{1,0:T(8,128)(2,1)S(1)}, u32[]{:S(2)}, u32[]{:S(2)}) %collective-permute-start.1) | collective-permute-done | bytes 79904 | tf_op jit(solution)/shard_map/ppermute | solution.py:72
  14.6 2.5 %collective-permute-start.12 = (bf16[40,1664]{1,0:T(8,128)(2,1)S(1)}, bf16[40,1664]{1,0:T(8,128)(2,1)S(1)}, u32[]{:S(2)}, u32[]{:S(2)}) collective-permute-start(bf16[40,1664]{1,0:T(8,128)(2,1)S(1)} %get-tuple-element.62._.refs_0_), channel_id=1, source_target_pairs={{0,24},{8,16},{16,8},{24,0},{1,25},{9,17},{17,9},{25,1},{2,26},{10... | collective-permute-start | bytes 399368 | tf_op jit(solution)/shard_map/ppermute | solution.py:72
  18.1 2.5 %collective-permute-start.5 = (bf16[40,1664]{1,0:T(8,128)(2,1)S(1)}, bf16[40,1664]{1,0:T(8,128)(2,1)S(1)}, u32[]{:S(2)}, u32[]{:S(2)}) collective-permute-start(bf16[40,1664]{1,0:T(8,128)(2,1)S(1)} %get-tuple-element.57.refs_0_), channel_id=1, source_target_pairs={{0,24},{8,16},{16,8},{24,0},{1,25},{9,17},{17,9},{25,1},{2,26},{10... | collective-permute-start | bytes 399368 | tf_op jit(solution)/shard_map/ppermute | solution.py:72
  21.1 1.0 %collective-permute-done.12.refs_3_ = bf16[40,1664]{1,0:T(8,128)(2,1)S(1)} collective-permute-done((bf16[40,1664]{1,0:T(8,128)(2,1)S(1)}, bf16[40,1664]{1,0:T(8,128)(2,1)S(1)}, u32[]{:S(2)}, u32[]{:S(2)}) %collective-permute-start.12) | collective-permute-done | bytes 133152 | tf_op jit(solution)/shard_map/ppermute | solution.py:72
  22.1 1.4 %collective-permute-start.3 = (bf16[40,1664]{1,0:T(8,128)(2,1)S(1)}, bf16[40,1664]{1,0:T(8,128)(2,1)S(1)}, u32[]{:S(2)}, u32[]{:S(2)}) collective-permute-start(bf16[40,1664]{1,0:T(8,128)(2,1)S(1)} %get-tuple-element.57.refs_0_), channel_id=1, source_target_pairs={{0,8},{8,0},{16,24},{24,16},{1,9},{9,1},{17,25},{25,17},{2,10},{10... | collective-permute-start | bytes 399368 | tf_op jit(solution)/shard_map/ppermute | solution.py:72
  23.5 2.0 %collective-permute-done.11.refs_2_ = bf16[40,1664]{1,0:T(8,128)(2,1)S(1)} collective-permute-done((bf16[40,1664]{1,0:T(8,128)(2,1)S(1)}, bf16[40,1664]{1,0:T(8,128)(2,1)S(1)}, u32[]{:S(2)}, u32[]{:S(2)}) %collective-permute-start.11) | collective-permute-done | bytes 133152 | tf_op jit(solution)/shard_map/ppermute | solution.py:72
  26.1 1.2 %collective-permute-done.5.refs_3_ = bf16[40,1664]{1,0:T(8,128)(2,1)S(1)} collective-permute-done((bf16[40,1664]{1,0:T(8,128)(2,1)S(1)}, bf16[40,1664]{1,0:T(8,128)(2,1)S(1)}, u32[]{:S(2)}, u32[]{:S(2)}) %collective-permute-start.5) | collective-permute-done | bytes 133152 | tf_op jit(solution)/shard_map/ppermute | solution.py:72
  27.2 0.9 %collective-permute-done.4.refs_2_ = bf16[40,1664]{1,0:T(8,128)(2,1)S(1)} collective-permute-done((bf16[40,1664]{1,0:T(8,128)(2,1)S(1)}, bf16[40,1664]{1,0:T(8,128)(2,1)S(1)}, u32[]{:S(2)}, u32[]{:S(2)}) %collective-permute-start.4) | collective-permute-done | bytes 133152 | tf_op jit(solution)/shard_map/ppermute | solution.py:72
  29.2 3.6 %shard_map.113 = (bf16[2,1024,1664]{2,1,0:T(8,128)(2,1)S(1)}, f32[8,128]{1,0:T(8,128)}) custom-call(bf16[4,1024,1664]{2,1,0:T(8,128)(2,1)} %refs_10_.1, bf16[40,1664]{1,0:T(8,128)(2,1)S(1)} %get-tuple-element.62._.refs_0_), custom_call_target="tpu_custom_call" | custom-call | bytes 6815744 | tf_op jit(solution)/shard_map/pallas_call | solution.py:46
  32.9 4.4 %shard_map.114 = (bf16[5,64,1664]{2,1,0:T(8,128)(2,1)S(1)}, f32[5,64,1024]{2,1,0:T(8,128)S(1)}, bf16[5,64,1024]{2,1,0:T(8,128)(2,1)S(1)}, f32[8,128]{1,0:T(8,128)}) custom-call(s32[16]{0:T(128)S(1)} %copy-done.1, bf16[40,1664]{1,0:T(8,128)(2,1)S(1)} %get-tuple-element.62._.refs_0_, bf16[40,1664]{1,0:T(8,128)(2,1)S(1)} %collective-permute-done.10.refs_1_, ...), custom_call_target="tpu_custom_call" | custom-call | bytes 16777216 | tf_op jit(solution)/shard_map/pallas_call | solution.py:46
  37.3 1.9 %shard_map.115.refs_13_ = bf16[5,64,1664]{2,1,0:T(8,128)(2,1)S(1)} custom-call(s32[16]{0:T(128)S(1)} %copy-done.1, bf16[2,1024,1664]{2,1,0:T(8,128)(2,1)S(1)} %get-tuple-element.63.refs_9_.w, bf16[5,64,1024]{2,1,0:T(8,128)(2,1)S(1)} %get-tuple-element.68.hid_ref.refs_12_.refs_0_), custom_call_target="tpu_custom_call" | custom-call | bytes 8388608 | tf_op jit(solution)/shard_map/pallas_call | solution.py:46
  39.3 11.9 %shard_map.116 = (bf16[5,64,1664]{2,1,0:T(8,128)(2,1)S(1)}, bf16[5,64,1024]{2,1,0:T(8,128)(2,1)S(1)}, bf16[4,80,1664]{2,1,0:T(8,128)(2,1)S(1)}, bf16[4,80,1664]{2,1,0:T(8,128)(2,1)S(1)}, f32[4,1024,1664]{2,1,0:T(8,128)}) custom-call(s32[16]{0:T(128)S(1)} %copy-done.1, bf16[40,1664]{1,0:T(8,128)(2,1)S(1)} %get-tuple-element.57.refs_0_, ...), custom_call_target="tpu_custom_call" | custom-call | bytes 50331648 | tf_op jit(solution)/shard_map/pallas_call | solution.py:46
  51.7 2.8 %shard_map.117 = (f32[4,1024,1664]{2,1,0:T(8,128)}, f32[8,128]{1,0:T(8,128)S(1)}) custom-call(s32[16]{0:T(128)S(1)} %copy-done.1, bf16[5,64,1024]{2,1,0:T(8,128)(2,1)S(1)} %get-tuple-element.68.hid_ref.refs_12_.refs_0_, bf16[5,64,1664]{2,1,0:T(8,128)(2,1)S(1)} %get-tuple-element.71.refs_1_, ...), custom_call_target="tpu_custom_call", output_to_operand_aliasing={{0}: (3, {})} | custom-call | bytes 6815744 | tf_op jit(solution)/shard_map/pallas_call | solution.py:46
  54.7 1.0 %collective-permute-start.18 = (bf16[80,1664]{1,0:T(8,128)(2,1)S(1)}, bf16[80,1664]{1,0:T(8,128)(2,1)S(1)}, u32[]{:S(2)}, u32[]{:S(2)}) collective-permute-start(bf16[80,1664]{1,0:T(8,128)(2,1)S(1)} %get-tuple-element.75), channel_id=1, source_target_pairs={{0,8},{8,0},{16,24},{24,16},{1,9},{9,1},{17,25},{25,17},{2,10},{10... | collective-permute-start | bytes 798728 | tf_op jit(solution)/shard_map/ppermute | solution.py:72
  56.5 1.8 %collective-permute-start.20 = (bf16[80,1664]{1,0:T(8,128)(2,1)S(1)}, bf16[80,1664]{1,0:T(8,128)(2,1)S(1)}, u32[]{:S(2)}, u32[]{:S(2)}) collective-permute-start(bf16[80,1664]{1,0:T(8,128)(2,1)S(1)} %get-tuple-element.77), channel_id=1, source_target_pairs={{0,24},{8,16},{16,8},{24,0},{1,25},{9,17},{17,9},{25,1},{2,26},{10... | collective-permute-start | bytes 798728 | tf_op jit(solution)/shard_map/ppermute | solution.py:72
  58.2 11.1 %shard_map.119 = (f32[4,1024,1664]{2,1,0:T(8,128)}, f32[4,1664,1024]{2,1,0:T(8,128)}, f32[8,128]{1,0:T(8,128)S(1)}) custom-call(s32[16]{0:T(128)S(1)} %copy-done.1, bf16[5,64,1024]{2,1,0:T(8,128)(2,1)S(1)} %get-tuple-element.68.hid_ref.refs_12_.refs_0_, bf16[5,64,1664]{2,1,0:T(8,128)(2,1)S(1)} %get-tuple-element.71.refs_1_, ...), custom_call_target="tpu_custom_call", output_to_operand_aliasing={{0}: (5, {})} | custom-call | bytes 34078720 | tf_op jit(solution)/shard_map/pallas_call | solution.py:46
  69.9 2.3 %collective-permute-start.21 = (bf16[24,1664]{1,0:T(8,128)(2,1)S(1)}, bf16[24,1664]{1,0:T(8,128)(2,1)S(1)}, u32[]{:S(2)}, u32[]{:S(2)}) collective-permute-start(bf16[24,1664]{1,0:T(8,128)(2,1)S(1)} %get-tuple-element.83), channel_id=1, source_target_pairs={{0,2},{2,0},{4,6},{6,4},{1,3},{3,1},{5,7},{7,5},{8,10},{10,8},{12,... | collective-permute-start | bytes 239624 | tf_op jit(solution)/shard_map/ppermute | solution.py:72
  72.2 1.6 %collective-permute-start.22 = (bf16[24,1664]{1,0:T(8,128)(2,1)S(1)}, bf16[24,1664]{1,0:T(8,128)(2,1)S(1)}, u32[]{:S(2)}, u32[]{:S(2)}) collective-permute-start(bf16[24,1664]{1,0:T(8,128)(2,1)S(1)} %get-tuple-element.84), channel_id=1, source_target_pairs={{0,4},{2,6},{4,0},{6,2},{1,5},{3,7},{5,1},{7,3},{8,12},{10,14},{12... | collective-permute-start | bytes 239624 | tf_op jit(solution)/shard_map/ppermute | solution.py:72
  74.6 6.1 %shard_map.121 = (f32[4,1664,1024]{2,1,0:T(8,128)}, f32[8,128]{1,0:T(8,128)S(1)}) custom-call(s32[16]{0:T(128)S(1)} %copy-done.1, bf16[5,64,1664]{2,1,0:T(8,128)(2,1)S(1)} %get-tuple-element.78.refs_2_.refs_0_, bf16[5,64,1024]{2,1,0:T(8,128)(2,1)S(1)} %get-tuple-element.79.refs_3_.refs_1_, ...), custom_call_target="tpu_custom_call", output_to_operand_aliasing={{0}: (3, {})} | custom-call | bytes 13631488 | tf_op jit(solution)/shard_map/pallas_call | solution.py:46
  80.8 1.0 %shard_map.122 = (bf16[32,1664]{1,0:T(8,128)(2,1)}, bf16[32,1664]{1,0:T(8,128)(2,1)}, f32[2,32]{1,0:T(2,128)}) custom-call(f32[2,32]{1,0:T(2,128)S(1)} %bitcast.6, bf16[32,1664]{1,0:T(8,128)(2,1)S(1)} %copy-done, bf16[96,32]{1,0:T(8,128)(2,1)S(1)} %get-tuple-element.49.t0, bf16[96,32]{1,0:T(8,128)(2,1)S(1)} %get-tuple-element.50.t1, ...), custom_call_target="tpu_custom_call" | custom-call | bytes 1048576 | tf_op jit(solution)/shard_map/pallas_call | solution.py:46
  (43 shorter events, 6.2 us)
Async XLA Ops:
  2.2 10.7 %collective-permute-start = (bf16[24,1664]{1,0:T(8,128)(2,1)S(1)}, bf16[24,1664]{1,0:T(8,128)(2,1)S(1)}, u32[]{:S(2)}, u32[]{:S(2)}) collective-permute-start(bf16[24,1664]{1,0:T(8,128)(2,1)S(1)} %get-tuple-element.53), channel_id=1, source_target_pairs={{0,2},{2,0},{4,6},{6,4},{1,3},{3,1},{5,7},{7,5},{8,10},{10,8},{12,... | collective-permute-start | bytes 239624 | tf_op jit(solution)/shard_map/ppermute | solution.py:72
  5.3 9.0 %collective-permute-start.1 = (bf16[24,1664]{1,0:T(8,128)(2,1)S(1)}, bf16[24,1664]{1,0:T(8,128)(2,1)S(1)}, u32[]{:S(2)}, u32[]{:S(2)}) collective-permute-start(bf16[24,1664]{1,0:T(8,128)(2,1)S(1)} %get-tuple-element.54), channel_id=1, source_target_pairs={{0,4},{2,6},{4,0},{6,2},{1,5},{3,7},{5,1},{7,3},{8,12},{10,14},{12... | collective-permute-start | bytes 239624 | tf_op jit(solution)/shard_map/ppermute | solution.py:72
  7.9 6.5 %collective-permute-start.2 = (bf16[24,1664]{1,0:T(8,128)(2,1)S(1)}, bf16[24,1664]{1,0:T(8,128)(2,1)S(1)}, u32[]{:S(2)}, u32[]{:S(2)}) collective-permute-start(bf16[24,1664]{1,0:T(8,128)(2,1)S(1)} %get-tuple-element.55), channel_id=1, source_target_pairs={{0,6},{2,4},{4,2},{6,0},{1,7},{3,5},{5,3},{7,1},{8,14},{10,12},{12... | collective-permute-start | bytes 239624 | tf_op jit(solution)/shard_map/ppermute | solution.py:72
  14.6 7.5 %collective-permute-start.12 = (bf16[40,1664]{1,0:T(8,128)(2,1)S(1)}, bf16[40,1664]{1,0:T(8,128)(2,1)S(1)}, u32[]{:S(2)}, u32[]{:S(2)}) collective-permute-start(bf16[40,1664]{1,0:T(8,128)(2,1)S(1)} %get-tuple-element.62._.refs_0_), channel_id=1, source_target_pairs={{0,24},{8,16},{16,8},{24,0},{1,25},{9,17},{17,9},{25,1},{2,26},{10... | collective-permute-start | bytes 399368 | tf_op jit(solution)/shard_map/ppermute | solution.py:72
  17.1 8.4 %collective-permute-start.11 = (bf16[40,1664]{1,0:T(8,128)(2,1)S(1)}, bf16[40,1664]{1,0:T(8,128)(2,1)S(1)}, u32[]{:S(2)}, u32[]{:S(2)}) collective-permute-start(bf16[40,1664]{1,0:T(8,128)(2,1)S(1)} %get-tuple-element.62._.refs_0_), channel_id=1, source_target_pairs={{0,16},{8,24},{16,0},{24,8},{1,17},{9,25},{17,1},{25,9},{2,18},{10... | collective-permute-start | bytes 399368 | tf_op jit(solution)/shard_map/ppermute | solution.py:72
  17.6 7.9 %collective-permute-start.10 = (bf16[40,1664]{1,0:T(8,128)(2,1)S(1)}, bf16[40,1664]{1,0:T(8,128)(2,1)S(1)}, u32[]{:S(2)}, u32[]{:S(2)}) collective-permute-start(bf16[40,1664]{1,0:T(8,128)(2,1)S(1)} %get-tuple-element.62._.refs_0_), channel_id=1, source_target_pairs={{0,8},{8,0},{16,24},{24,16},{1,9},{9,1},{17,25},{25,17},{2,10},{10... | collective-permute-start | bytes 399368 | tf_op jit(solution)/shard_map/ppermute | solution.py:72
  18.1 9.1 %collective-permute-start.5 = (bf16[40,1664]{1,0:T(8,128)(2,1)S(1)}, bf16[40,1664]{1,0:T(8,128)(2,1)S(1)}, u32[]{:S(2)}, u32[]{:S(2)}) collective-permute-start(bf16[40,1664]{1,0:T(8,128)(2,1)S(1)} %get-tuple-element.57.refs_0_), channel_id=1, source_target_pairs={{0,24},{8,16},{16,8},{24,0},{1,25},{9,17},{17,9},{25,1},{2,26},{10... | collective-permute-start | bytes 399368 | tf_op jit(solution)/shard_map/ppermute | solution.py:72
  20.6 7.5 %collective-permute-start.4 = (bf16[40,1664]{1,0:T(8,128)(2,1)S(1)}, bf16[40,1664]{1,0:T(8,128)(2,1)S(1)}, u32[]{:S(2)}, u32[]{:S(2)}) collective-permute-start(bf16[40,1664]{1,0:T(8,128)(2,1)S(1)} %get-tuple-element.57.refs_0_), channel_id=1, source_target_pairs={{0,16},{8,24},{16,0},{24,8},{1,17},{9,25},{17,1},{25,9},{2,18},{10... | collective-permute-start | bytes 399368 | tf_op jit(solution)/shard_map/ppermute | solution.py:72
  22.1 6.1 %collective-permute-start.3 = (bf16[40,1664]{1,0:T(8,128)(2,1)S(1)}, bf16[40,1664]{1,0:T(8,128)(2,1)S(1)}, u32[]{:S(2)}, u32[]{:S(2)}) collective-permute-start(bf16[40,1664]{1,0:T(8,128)(2,1)S(1)} %get-tuple-element.57.refs_0_), channel_id=1, source_target_pairs={{0,8},{8,0},{16,24},{24,16},{1,9},{9,1},{17,25},{25,17},{2,10},{10... | collective-permute-start | bytes 399368 | tf_op jit(solution)/shard_map/ppermute | solution.py:72
  25.5 3.1 %collective-permute-start.13 = (bf16[40,1664]{1,0:T(8,128)(2,1)S(1)}, bf16[40,1664]{1,0:T(8,128)(2,1)S(1)}, u32[]{:S(2)}, u32[]{:S(2)}) collective-permute-start(bf16[40,1664]{1,0:T(8,128)(2,1)S(1)} %get-tuple-element.62._.refs_0_), channel_id=1, source_target_pairs={{0,1},{1,0},{2,3},{3,2},{4,5},{5,4},{6,7},{7,6},{8,9},{9,8},{10,11... | collective-permute-start | bytes 399368 | tf_op jit(solution)/shard_map/ppermute | solution.py:72
  25.5 3.2 %collective-permute-start.14 = (bf16[40,1664]{1,0:T(8,128)(2,1)S(1)}, bf16[40,1664]{1,0:T(8,128)(2,1)S(1)}, u32[]{:S(2)}, u32[]{:S(2)}) collective-permute-start(bf16[40,1664]{1,0:T(8,128)(2,1)S(1)} %collective-permute-done.10.refs_1_), channel_id=1, source_target_pairs={{0,1},{1,0},{2,3},{3,2},{4,5},{5,4},{6,7},{7,6},{8,9},{9,8},{10,11... | collective-permute-start | bytes 399368 | tf_op jit(solution)/shard_map/ppermute | solution.py:72
  27.2 1.9 %collective-permute-start.15 = (bf16[40,1664]{1,0:T(8,128)(2,1)S(1)}, bf16[40,1664]{1,0:T(8,128)(2,1)S(1)}, u32[]{:S(2)}, u32[]{:S(2)}) collective-permute-start(bf16[40,1664]{1,0:T(8,128)(2,1)S(1)} %collective-permute-done.11.refs_2_), channel_id=1, source_target_pairs={{0,1},{1,0},{2,3},{3,2},{4,5},{5,4},{6,7},{7,6},{8,9},{9,8},{10,11... | collective-permute-start | bytes 399368 | tf_op jit(solution)/shard_map/ppermute | solution.py:72
  28.1 11.1 %collective-permute-start.6 = (bf16[40,1664]{1,0:T(8,128)(2,1)S(1)}, bf16[40,1664]{1,0:T(8,128)(2,1)S(1)}, u32[]{:S(2)}, u32[]{:S(2)}) collective-permute-start(bf16[40,1664]{1,0:T(8,128)(2,1)S(1)} %get-tuple-element.57.refs_0_), channel_id=1, source_target_pairs={{0,1},{1,0},{2,3},{3,2},{4,5},{5,4},{6,7},{7,6},{8,9},{9,8},{10,11... | collective-permute-start | bytes 399368 | tf_op jit(solution)/shard_map/ppermute | solution.py:72
  28.1 4.7 %collective-permute-start.16 = (bf16[40,1664]{1,0:T(8,128)(2,1)S(1)}, bf16[40,1664]{1,0:T(8,128)(2,1)S(1)}, u32[]{:S(2)}, u32[]{:S(2)}) collective-permute-start(bf16[40,1664]{1,0:T(8,128)(2,1)S(1)} %collective-permute-done.12.refs_3_), channel_id=1, source_target_pairs={{0,1},{1,0},{2,3},{3,2},{4,5},{5,4},{6,7},{7,6},{8,9},{9,8},{10,11... | collective-permute-start | bytes 399368 | tf_op jit(solution)/shard_map/ppermute | solution.py:72
  28.6 10.6 %collective-permute-start.7 = (bf16[40,1664]{1,0:T(8,128)(2,1)S(1)}, bf16[40,1664]{1,0:T(8,128)(2,1)S(1)}, u32[]{:S(2)}, u32[]{:S(2)}) collective-permute-start(bf16[40,1664]{1,0:T(8,128)(2,1)S(1)} %collective-permute-done.3.refs_1_), channel_id=1, source_target_pairs={{0,1},{1,0},{2,3},{3,2},{4,5},{5,4},{6,7},{7,6},{8,9},{9,8},{10,11... | collective-permute-start | bytes 399368 | tf_op jit(solution)/shard_map/ppermute | solution.py:72
  28.7 10.5 %collective-permute-start.8 = (bf16[40,1664]{1,0:T(8,128)(2,1)S(1)}, bf16[40,1664]{1,0:T(8,128)(2,1)S(1)}, u32[]{:S(2)}, u32[]{:S(2)}) collective-permute-start(bf16[40,1664]{1,0:T(8,128)(2,1)S(1)} %collective-permute-done.4.refs_2_), channel_id=1, source_target_pairs={{0,1},{1,0},{2,3},{3,2},{4,5},{5,4},{6,7},{7,6},{8,9},{9,8},{10,11... | collective-permute-start | bytes 399368 | tf_op jit(solution)/shard_map/ppermute | solution.py:72
  29.1 10.1 %collective-permute-start.9 = (bf16[40,1664]{1,0:T(8,128)(2,1)S(1)}, bf16[40,1664]{1,0:T(8,128)(2,1)S(1)}, u32[]{:S(2)}, u32[]{:S(2)}) collective-permute-start(bf16[40,1664]{1,0:T(8,128)(2,1)S(1)} %collective-permute-done.5.refs_3_), channel_id=1, source_target_pairs={{0,1},{1,0},{2,3},{3,2},{4,5},{5,4},{6,7},{7,6},{8,9},{9,8},{10,11... | collective-permute-start | bytes 399368 | tf_op jit(solution)/shard_map/ppermute | solution.py:72
  51.2 3.3 %collective-permute-start.17 = (bf16[4,80,1664]{2,1,0:T(8,128)(2,1)S(1)}, bf16[4,80,1664]{2,1,0:T(8,128)(2,1)S(1)}, u32[]{:S(2)}, u32[]{:S(2)}) collective-permute-start(bf16[4,80,1664]{2,1,0:T(8,128)(2,1)S(1)} %get-tuple-element.70.refs_3_), channel_id=1, source_target_pairs={{0,1},{1,0},{2,3},{3,2},{4,5},{5,4},{6,7},{7,6},{8,9},{9,8},{10,11... | collective-permute-start | bytes 3194888 | tf_op jit(solution)/shard_map/ppermute | solution.py:72
  54.7 14.6 %collective-permute-start.18 = (bf16[80,1664]{1,0:T(8,128)(2,1)S(1)}, bf16[80,1664]{1,0:T(8,128)(2,1)S(1)}, u32[]{:S(2)}, u32[]{:S(2)}) collective-permute-start(bf16[80,1664]{1,0:T(8,128)(2,1)S(1)} %get-tuple-element.75), channel_id=1, source_target_pairs={{0,8},{8,0},{16,24},{24,16},{1,9},{9,1},{17,25},{25,17},{2,10},{10... | collective-permute-start | bytes 798728 | tf_op jit(solution)/shard_map/ppermute | solution.py:72
  55.7 13.8 %collective-permute-start.19 = (bf16[80,1664]{1,0:T(8,128)(2,1)S(1)}, bf16[80,1664]{1,0:T(8,128)(2,1)S(1)}, u32[]{:S(2)}, u32[]{:S(2)}) collective-permute-start(bf16[80,1664]{1,0:T(8,128)(2,1)S(1)} %get-tuple-element.76), channel_id=1, source_target_pairs={{0,16},{8,24},{16,0},{24,8},{1,17},{9,25},{17,1},{25,9},{2,18},{10... | collective-permute-start | bytes 798728 | tf_op jit(solution)/shard_map/ppermute | solution.py:72
  56.5 13.1 %collective-permute-start.20 = (bf16[80,1664]{1,0:T(8,128)(2,1)S(1)}, bf16[80,1664]{1,0:T(8,128)(2,1)S(1)}, u32[]{:S(2)}, u32[]{:S(2)}) collective-permute-start(bf16[80,1664]{1,0:T(8,128)(2,1)S(1)} %get-tuple-element.77), channel_id=1, source_target_pairs={{0,24},{8,16},{16,8},{24,0},{1,25},{9,17},{17,9},{25,1},{2,26},{10... | collective-permute-start | bytes 798728 | tf_op jit(solution)/shard_map/ppermute | solution.py:72
  69.9 10.9 %collective-permute-start.21 = (bf16[24,1664]{1,0:T(8,128)(2,1)S(1)}, bf16[24,1664]{1,0:T(8,128)(2,1)S(1)}, u32[]{:S(2)}, u32[]{:S(2)}) collective-permute-start(bf16[24,1664]{1,0:T(8,128)(2,1)S(1)} %get-tuple-element.83), channel_id=1, source_target_pairs={{0,2},{2,0},{4,6},{6,4},{1,3},{3,1},{5,7},{7,5},{8,10},{10,8},{12,... | collective-permute-start | bytes 239624 | tf_op jit(solution)/shard_map/ppermute | solution.py:72
  72.2 8.6 %collective-permute-start.22 = (bf16[24,1664]{1,0:T(8,128)(2,1)S(1)}, bf16[24,1664]{1,0:T(8,128)(2,1)S(1)}, u32[]{:S(2)}, u32[]{:S(2)}) collective-permute-start(bf16[24,1664]{1,0:T(8,128)(2,1)S(1)} %get-tuple-element.84), channel_id=1, source_target_pairs={{0,4},{2,6},{4,0},{6,2},{1,5},{3,7},{5,1},{7,3},{8,12},{10,14},{12... | collective-permute-start | bytes 239624 | tf_op jit(solution)/shard_map/ppermute | solution.py:72
  73.8 6.9 %collective-permute-start.23 = (bf16[24,1664]{1,0:T(8,128)(2,1)S(1)}, bf16[24,1664]{1,0:T(8,128)(2,1)S(1)}, u32[]{:S(2)}, u32[]{:S(2)}) collective-permute-start(bf16[24,1664]{1,0:T(8,128)(2,1)S(1)} %get-tuple-element.85), channel_id=1, source_target_pairs={{0,6},{2,4},{4,2},{6,0},{1,7},{3,5},{5,3},{7,1},{8,14},{10,12},{12... | collective-permute-start | bytes 239624 | tf_op jit(solution)/shard_map/ppermute | solution.py:72
  (3 other events, 37.2 us)
